TPU v7x, 1024 devices: a whole 4x4x32 slice. The times are simulated.
1024 devices in a mesh: row: 64 (over z, core), col: 16 (over y, x).
Axes of the slice: x: 4, y: 4, z: 32, core: 2. Of those that a mesh axis runs over, the one named last changes fastest.
Arguments:
- depth: float32 [4096, 2048], P('row', 'col'), may hold values from 0 to 12, as said below
- elevation: float32 [4096, 2048], P('row', 'col'), may hold values from -4 to 4
- flow_x: float32 [4096, 2048], P('row', 'col'), may hold values from -3 to 3
- flow_y: float32 [4096, 2048], P('row', 'col'), may hold values from -3 to 3
- wet_mask: int32 [4096, 2048], P('row', 'col'), may hold values 0 or 1
- manning_class: int32 [4096, 2048], P('row', 'col'), may hold values from 0 to 7
- manning_table: float32 [8], replicated, may hold values from 0.02 to 0.2
Outputs:
- depth_out: float32 [4096, 2048], P('row', 'col')
- flow_x_out: float32 [4096, 2048], P('row', 'col')
- flow_y_out: float32 [4096, 2048], P('row', 'col')
Inputs may be any that keep to these rules, and one draw needn't show every extreme that they name: `depth`: depth is 0 or positive.
All inputs are finite; a program needn't handle non-finite values. No bound on the sum of `wet_mask` on one device may be relied on, other than what follows from the above.
Results may differ from a plain program's by a relative error of at most 0.000033.
Values sent between devices are 32-bit elements; how exact they have to be, the bound alone decides.
No kernel may reach another device: no remote copies, remote signals or barrier semaphores. Data moves between devices by JAX's collectives and lax.ppermute only.
A program may use at most 32 MiB of HBM per device.

v0:
```python
import jax
import jax.numpy as jnp
from jax import lax
from jax.experimental import pallas as pl
from jax.experimental.pallas import tpu as pltpu
from jax.sharding import PartitionSpec as P

ITERS = 12
CLASSES = 8
HALO = ITERS

GRAVITY = 9.81
SPACING = 30.0
COURANT = 0.7
DRY_FLOOR = 0.01
FLOW_FLOOR = 0.05

ROW = ("z", "core")

REACH = 4
FIELDS = 6
KEYS = ITERS


def note_places():
    room = [ITERS + REACH]
    places = {}
    for window in range(REACH, 0, -1):
        span = FIELDS * (2 * window + 1)
        for row in range(window + 1):
            tile = next((t for t, used in enumerate(room) if used + span <= 128), len(room))
            if tile == len(room):
                room.append(0)
            places[window, row] = (tile, room[tile])
            room[tile] += span
    return places, len(room)


PLACES, TILES = note_places()
NOTE = 128 * TILES


def neighbours(axis):
    peers = lax.axis_size(axis)
    up = [(i, i + 1) for i in range(peers - 1)]
    down = [(j, i) for i, j in up]
    return up, down


def with_halo(fields):
    rows, cols = fields.shape[1:]
    up, down = neighbours(ROW)
    before = lax.ppermute(fields[:, rows - HALO :], ROW, up)
    after = lax.ppermute(fields[:, :HALO], ROW, down)
    fields = jnp.concatenate([fields, after, before], axis=1)
    up, down = neighbours("col")
    before = lax.ppermute(fields[:, :, cols - HALO :], "col", up)
    after = lax.ppermute(fields[:, :, :HALO], "col", down)
    gap = jnp.zeros((*fields.shape[:2], cols - 2 * HALO), fields.dtype)
    return jnp.concatenate([fields, after, gap, before], axis=2)


def next_of(x, axis):
    return pltpu.roll(x, x.shape[axis] - 1, axis)


def previous_of(x, axis):
    return pltpu.roll(x, 1, axis)


def step_of(deepest):
    return COURANT * SPACING / jnp.sqrt(GRAVITY * jnp.maximum(deepest, DRY_FLOOR))


def fixed_parts(bed, opening):
    return tuple(
        (jnp.maximum(bed, next_of(bed, axis)), opening * next_of(opening, axis)) for axis in (0, 1)
    )


def face_flux(flow_old, surface, surf_high, bed_max, rough, opening, time_step):
    flow_depth = jnp.maximum(surface, surf_high) - bed_max
    driving = jnp.maximum(flow_depth, 0.0)
    friction_depth = jnp.maximum(flow_depth, FLOW_FLOOR)
    slope = (surf_high - surface) / SPACING
    driven = flow_old - GRAVITY * driving * time_step * slope
    damping = 1.0 + GRAVITY * time_step * rough * jnp.abs(flow_old) * jnp.exp(
        -7.0 / 3.0 * jnp.log(friction_depth)
    )
    return opening * driven / damping


def advance(depth, flow_x, flow_y, bed, rough, faces, time_step):
    surface = depth + bed
    (bed_x, open_x), (bed_y, open_y) = faces
    rows_new = face_flux(flow_x, surface, next_of(surface, 0), bed_x, rough, open_x, time_step)
    cols_new = face_flux(flow_y, surface, next_of(surface, 1), bed_y, rough, open_y, time_step)
    change = previous_of(rows_new, 0) - rows_new + (previous_of(cols_new, 1) - cols_new)
    return jnp.maximum(depth + time_step / SPACING * change, 0.0), rows_new, cols_new


def lanes_of(shape):
    return lax.broadcasted_iota(jnp.int32, shape, len(shape) - 1)


def rows_of(shape):
    return lax.broadcasted_iota(jnp.int32, shape, len(shape) - 2)


def total(x, how):
    return how(how(x, axis=0, keepdims=True), axis=1, keepdims=True)


def merged(notes):
    head = notes[:, :128]
    lane = lanes_of(head.shape)
    out_lane = lanes_of((1, NOTE))
    place = rows_of((notes.shape[0], 1)).astype(jnp.float32)
    out = jnp.max(notes, axis=0, keepdims=True)
    for window in range(1, REACH + 1):
        keyed = jnp.max(jnp.where(lane == KEYS + window - 1, head, -1.0), axis=1, keepdims=True)
        best = keyed == jnp.max(keyed, axis=0, keepdims=True)
        first = jnp.min(jnp.where(best, place, 1e6), axis=0, keepdims=True)
        chosen = jnp.sum(jnp.where(place == first, notes, 0.0), axis=0, keepdims=True)
        for row in range(window + 1):
            tile, at = PLACES[window, row]
            start = 128 * tile + at
            here = (out_lane >= start) & (out_lane < start + FIELDS * (2 * window + 1))
            out = jnp.where(here, chosen, out)
    return out


def merge_kernel(notes, out):
    out[...] = jnp.broadcast_to(merged(notes[:, 0, :])[:, None, :], out.shape)


def turned(x, shift, axis):
    size = x.shape[axis]
    return pltpu.roll(x, shift % size, axis) if shift % size else x


def window_shape(window):
    return (8 if 2 * window < 8 else 16, 128)


def columns_of(shape, width):
    lane = lanes_of(shape)
    column = lane
    for f in range(1, FIELDS):
        column = jnp.where(lane >= width * f, lane - width * f, column)
    return column


def window_fields(note, window):
    width = 2 * window + 1
    shape = window_shape(window)
    row, lane = rows_of(shape), lanes_of(shape)
    column = columns_of(shape, width)
    folded = jnp.zeros(shape, jnp.float32)
    for i in range(window + 1):
        tile, at = PLACES[window, i]
        line = turned(note[:, 128 * tile : 128 * (tile + 1)], -at, 1)
        folded = jnp.where(row == i, jnp.broadcast_to(line, shape), folded)
    lower = turned(folded, window + 1, 0)
    lower = jnp.where(column <= window, turned(lower, -window, 1), turned(lower, window + 1, 1))
    packed = jnp.where(row <= window, folded, lower)
    inside = jnp.abs(column - window) + jnp.abs(row - window) <= window
    packed = jnp.where(inside, packed, 0.0)
    return [jnp.where(lane < width, turned(packed, -width * f, 1), 0.0) for f in range(FIELDS)]


def window_lines(saved, at_row, at_col, window):
    width = 2 * window + 1
    shape = window_shape(window)
    row, lane = rows_of(shape), lanes_of(shape)
    column = columns_of(shape, width)
    packed = jnp.zeros(shape, jnp.float32)
    top = at_row + 8 - window
    off = lax.rem(top, 8)
    height = shape[0] + 8
    for f in range(FIELDS):
        strip = saved[f, pl.ds(pl.multiple_of(top - off, 8), height), :]
        strip = pltpu.roll(strip, lax.rem(height - off, height), 0)[: shape[0]]
        shift = lax.rem(width * f + window - at_col + 2 * 256, 256)
        moved = pltpu.roll(strip, shift, 1)[:, :128]
        packed = jnp.where((lane >= width * f) & (lane < width * (f + 1)), moved, packed)
    lower = turned(packed, -(window + 1), 0)
    lower = jnp.where(column > window, turned(lower, window, 1), turned(lower, -(window + 1), 1))
    folded = jnp.where(jnp.abs(column - window) <= row, packed, lower)
    return [folded[i : i + 1] for i in range(window + 1)]


def run_kernel(tile, first, certain, *refs):
    if first:
        fields, depth_out, flow_x_out, flow_y_out, note_out, guess_out, known_out = refs[:7]
    else:
        notes, guess_in, known_in, fields, depth_out, flow_x_out, flow_y_out, note_out, guess_out, known_out = refs[:10]
    state, faces, saved, guesses, depths, spots = refs[-6:]
    rows, cols = tile
    line_lane = lanes_of((1, 128))

    if first:
        known = jnp.int32(-1)
        guess_out[...] = jnp.full((1, 128), -1.0, jnp.float32)
    else:
        note = merged(notes[:, 0, :])
        true = note[:, :128]
        old = guess_in[...]
        wrong = jnp.where((true != old) & (line_lane < ITERS), line_lane.astype(jnp.float32), 1.0 * ITERS)
        miss = jnp.min(wrong).astype(jnp.int32)
        before = known_in[0]
        held = miss > before
        guess = true
        windows = {w: window_fields(note, w) for w in range(1, REACH + 1)}
        walls = {w: fixed_parts(parts[3], parts[5]) for w, parts in windows.items()}
        moving = {w: parts[:3] for w, parts in windows.items()}
        for stage in range(1, REACH + 1):
            level = jnp.max(jnp.where(line_lane == before + stage, guess, 0.0), axis=1, keepdims=True)
            time_step = step_of(level)
            for w in range(stage, REACH + 1):
                moving[w] = advance(*moving[w], windows[w][3], windows[w][4], walls[w], time_step)
            shape = window_shape(stage)
            here = (rows_of(shape) == stage) & (lanes_of(shape) == stage)
            centre = total(jnp.where(here, moving[stage][0], 0.0), jnp.max)
            target = before + stage + 1
            use = held & (target > miss) & (line_lane == target) & (centre > 0.0)
            guess = jnp.where(use, centre, guess)
        known = miss
        if not certain:
            known = jnp.where(held, jnp.maximum(before + REACH + 1, miss), miss)
        guess_out[...] = guess
        square = (16, 128)
        onto = rows_of(square) == lanes_of(square)
        spread = jnp.sum(jnp.where(onto, jnp.broadcast_to(guess, square), 0.0), axis=1, keepdims=True)
        guesses[...] = jnp.broadcast_to(spread, square)
    known_out[0] = known

    for f in range(3):
        state[f] = fields[f]
    bed, rough, opening = fields[3], fields[4], fields[5]
    for axis, (bed_max, both) in enumerate(fixed_parts(bed, opening)):
        faces[2 * axis] = bed_max
        faces[2 * axis + 1] = both
    last = fields.shape[1] - 8
    for f in range(3, FIELDS):
        saved[f, :8] = fields[f, last:]
        saved[f, 8:] = fields[f]
    depths[...] = jnp.full(depths.shape, -1.0, jnp.float32)

    def one_step(step, carry):
        depth, flow_x, flow_y = state[0], state[1], state[2]
        own = depth[:rows, :cols]
        deepest = total(own, jnp.max)
        depths[pl.ds(step, 1), :] = jnp.broadcast_to(deepest, (1, 128))

        @pl.when(step == known + 1)
        def _():
            for f in range(3):
                saved[f, :8] = state[f, last:]
                saved[f, 8:] = state[f]

        for j in range(REACH):

            @pl.when(step == known + 2 + j)
            def _():
                cell = (rows_of((rows, cols)) * cols + lanes_of((rows, cols))).astype(jnp.float32)
                spots[j] = jnp.min(jnp.where(own == deepest, cell, 1.0 * (rows * cols - 1))).astype(jnp.int32)

        level = deepest if first else guesses[pl.ds(step, 1), :][:, :1]
        new = advance(
            depth,
            flow_x,
            flow_y,
            fields[3],
            fields[4],
            ((faces[0], faces[1]), (faces[2], faces[3])),
            step_of(level),
        )
        for f in range(3):
            state[f] = new[f]
        return carry

    for j in range(REACH):
        spots[j] = 0
    lax.fori_loop(0, ITERS, one_step, 0)
    depth_out[...] = state[0, :rows, :cols]
    flow_x_out[...] = state[1, :rows, :cols]
    flow_y_out[...] = state[2, :rows, :cols]

    square = depths.shape
    onto = rows_of(square) == lanes_of(square)
    low = jnp.sum(jnp.where(onto, depths[...], 0.0), axis=0, keepdims=True)
    note = [low] + [jnp.zeros((1, 128), jnp.float32)] * (TILES - 1)
    for j in range(REACH):
        window = j + 1
        key = jnp.max(jnp.where(line_lane == known + 1 + window, low, -1.0), axis=1, keepdims=True)
        note[0] = jnp.where(line_lane == KEYS + j, key, note[0])
        lines = window_lines(saved, spots[j] // cols, lax.rem(spots[j], cols), window)
        for i, line in enumerate(lines):
            tile, at = PLACES[window, i]
            here = (line_lane >= at) & (line_lane < at + FIELDS * (2 * window + 1))
            note[tile] = jnp.where(here, turned(line, at, 1), note[tile])
    note = jnp.concatenate(note, axis=1)
    note_out[...] = jnp.broadcast_to(note[:, None, :], note_out.shape)


def per_device(depth, elevation, flow_x, flow_y, wet_mask, manning_class, manning_table):
    rough_sq = jnp.zeros(depth.shape, jnp.float32)
    for class_id in range(CLASSES):
        rough_sq = rough_sq + jnp.where(
            manning_class == class_id, manning_table[class_id] * manning_table[class_id], 0.0
        )
    wet_open = wet_mask.astype(jnp.float32)
    tile = depth.shape
    plane = ("core", "col")
    near_peers, far_peers = lax.axis_size("core") * lax.axis_size("col"), lax.axis_size("z")
    fields = with_halo(jnp.stack([depth, flow_x, flow_y, elevation, rough_sq, wet_open]))
    large = fields.shape[1:]

    def f32(*shape):
        return jax.ShapeDtypeStruct(shape, jnp.float32)

    merge = pl.pallas_call(merge_kernel, out_shape=f32(far_peers, 1, NOTE), name="merge_notes")

    def everywhere(note):
        over_plane = lax.all_to_all(note, plane, 0, 0, tiled=True)
        return lax.all_to_all(merge(over_plane), "z", 0, 0, tiled=True)

    def run(first, certain=False):
        vmem = pl.BlockSpec(memory_space=pltpu.VMEM)
        smem = pl.BlockSpec(memory_space=pltpu.SMEM)
        return pl.pallas_call(
            lambda *refs: run_kernel(tile, first, certain, *refs),
            in_specs=[vmem] if first else [vmem, vmem, smem, vmem],
            out_shape=(
                f32(*tile),
                f32(*tile),
                f32(*tile),
                f32(near_peers, 1, NOTE),
                f32(1, 128),
                jax.ShapeDtypeStruct((1,), jnp.int32),
            ),
            out_specs=(vmem, vmem, vmem, vmem, vmem, smem),
            scratch_shapes=[
                pltpu.VMEM((3, *large), jnp.float32),
                pltpu.VMEM((4, *large), jnp.float32),
                pltpu.VMEM((FIELDS, large[0] + 8, large[1]), jnp.float32),
                pltpu.VMEM((16, 128), jnp.float32),
                pltpu.VMEM((16, 128), jnp.float32),
                pltpu.SMEM((REACH,), jnp.int32),
            ],
            name="first_run" if first else "certain_run" if certain else "later_run",
        )

    def settled(notes, guess):
        true = jnp.max(notes[:, 0, :ITERS], axis=0)
        return jnp.all(true == guess[0, :ITERS])

    *result, note, guess, known = run(True)(fields)
    certain, later = run(False, True), run(False)
    for again in (certain, certain, later):
        *result, note, guess, known = again(everywhere(note), guess, known, fields)
    notes = everywhere(note)

    def unsettled(carry):
        return jnp.logical_not(carry[1]) & (carry[0] <= ITERS)

    def one_round(carry):
        count, _, notes, guess, known, _ = carry
        *result, note, guess, known = later(notes, guess, known, fields)
        notes = everywhere(note)
        return count + 1, settled(notes, guess), notes, guess, known, tuple(result)

    carry = (jnp.int32(0), settled(notes, guess), notes, guess, known, tuple(result))
    return lax.while_loop(unsettled, one_round, carry)[-1]


def solution(mesh):
    rows, cols = mesh.devices.shape
    split = jax.sharding.Mesh(mesh.devices.reshape(rows // 2, 2, cols), (*ROW, "col"))
    block = P(ROW, "col")
    return jax.shard_map(
        per_device,
        mesh=split,
        in_specs=(block, block, block, block, block, block, P()),
        out_specs=(block, block, block),
        check_vma=False,
    )
```

profile of v0, /device:TPU:1, one launch (start us, length us, event | category | flops | bytes accessed | tf_op | source)
XLA Modules:
  0.0 334.4 jit_solution(2676278401017879969)
XLA Ops:
  0.6 0.0 copy-start
  0.6 1.6 fusion.2
  12.2 0.0 copy-done
  12.2 0.0 copy-start.1
  12.3 0.7 copy-done.1
  13.0 0.0 copy-start.2
  13.0 0.8 copy-done.2
  13.8 0.0 copy-start.3
  13.8 0.8 copy-done.3
  14.5 0.0 copy-start.4
  14.5 0.8 copy-done.4
  15.3 0.0 copy-start.5
  15.3 0.7 copy-done.5
  16.1 16.0 %collective-permute-start = (f32[6,12,128]{2,1,0:T(8,128)S(1)}, f32[6,12,128]{2,1,0:T(8,128)S(1)}, u32[]{:S(2)}, u32[]{:S(2)}) collective-permute-start(f32[6,12,128]{2,1,0:T(8,128)S(1)} %get-tuple-element.108), channel_id=1, source_target_pairs={{16,0},{32,16},{48,32},{64,48},{80,64},{96,80},{112,96},{128,112},... | collective-permute-start | bytes 110600 | tf_op jit(solution)/shard_map/ppermute | solution.py:54
  32.1 1.9 collective-permute-start.1
  34.0 0.0 collective-permute-done
  34.0 1.2 collective-permute-done.1
  35.2 0.1 fusion
  35.4 1.3 collective-permute-start.2
  36.7 4.0 %collective-permute-start.3 = (f32[6,88,12]{2,1,0:T(8,128)S(1)}, f32[6,88,12]{2,1,0:T(8,128)S(1)}, u32[]{:S(2)}, u32[]{:S(2)}) collective-permute-start(f32[6,88,12]{2,1,0:T(8,128)S(1)} %get-tuple-element.107), channel_id=1, source_target_pairs={{0,1},{1,2},{2,3},{3,4},{4,5},{5,6},{6,7},{7,8},{8,9},{9,10},{10,1... | collective-permute-start | bytes 76040 | tf_op jit(solution)/shard_map/ppermute | solution.py:57
  40.7 0.1 pad.4.clone
  40.8 4.4 %collective-permute-done.2 = f32[6,88,12]{2,1,0:T(8,128)S(1)} collective-permute-done((f32[6,88,12]{2,1,0:T(8,128)S(1)}, f32[6,88,12]{2,1,0:T(8,128)S(1)}, u32[]{:S(2)}, u32[]{:S(2)}) %collective-permute-start.2) | collective-permute-done | bytes 25376 | tf_op jit(solution)/shard_map/ppermute | solution.py:58
  45.2 0.9 collective-permute-done.3
  46.1 0.1 pad_maximum_fusion.refs_0_.refs_3_
  46.2 5.8 %first_run.1 = (f32[64,128]{1,0:T(8,128)}, f32[64,128]{1,0:T(8,128)}, f32[64,128]{1,0:T(8,128)}, f32[32,1,640]{2,1,0:T(1,128)}, f32[1,128]{1,0:T(1,128)}, /*index=5*/s32[1]{0:T(128)}) custom-call(f32[6,88,256]{2,1,0:T(8,128)S(1)} %pad_maximum_fusion.refs_0_.refs_3_), custom_call_target="tpu_custom_call" | custom-call | tf_op jit(solution)/shard_map/first_run/pallas_call | solution.py:359
  52.1 12.8 %all_to_all.52.notes = f32[32,1,640]{2,1,0:T(1,128)} all-to-all(f32[32,1,640]{2,1,0:T(1,128)} %get-tuple-element.70), channel_id=1, replica_groups=mesh['z'=32,'core'=2,'col'=16] {'core','col'}, dimensions={0} | all-to-all | bytes 163840 | tf_op jit(solution)/shard_map/all_to_all | solution.py:326
  64.9 1.7 merge_notes.5
  66.6 48.4 %all_to_all.53.refs_0_ = f32[32,1,640]{2,1,0:T(1,128)} all-to-all(f32[32,1,640]{2,1,0:T(1,128)} %merge_notes.5), channel_id=1, replica_groups=mesh['z'=32,'core'=2,'col'=16] {'z'}, dimensions={0} | all-to-all | bytes 163840 | tf_op jit(solution)/shard_map/all_to_all | solution.py:327
  115.0 8.6 %certain_run.2 = (f32[64,128]{1,0:T(8,128)}, f32[64,128]{1,0:T(8,128)}, f32[64,128]{1,0:T(8,128)}, f32[32,1,640]{2,1,0:T(1,128)}, f32[1,128]{1,0:T(1,128)}, /*index=5*/s32[1]{0:T(128)}) custom-call(f32[32,1,640]{2,1,0:T(1,128)} %all_to_all.53.refs_0_, f32[1,128]{1,0:T(1,128)} %get-tuple-element.71.refs_1_, s32[1]{0:T(128)} %get-tuple-element.72.refs_2_, ...), custom_call_target="tpu_custom_call" | custom-call | tf_op jit(solution)/shard_map/certain_run/pallas_call | solution.py:362
  123.6 14.2 %all_to_all.54.notes = f32[32,1,640]{2,1,0:T(1,128)} all-to-all(f32[32,1,640]{2,1,0:T(1,128)} %get-tuple-element.73), channel_id=1, replica_groups=mesh['z'=32,'core'=2,'col'=16] {'core','col'}, dimensions={0} | all-to-all | bytes 163840 | tf_op jit(solution)/shard_map/all_to_all | solution.py:326
  137.9 1.7 merge_notes.6
  139.5 30.4 %all_to_all.55.refs_0_ = f32[32,1,640]{2,1,0:T(1,128)} all-to-all(f32[32,1,640]{2,1,0:T(1,128)} %merge_notes.6), channel_id=1, replica_groups=mesh['z'=32,'core'=2,'col'=16] {'z'}, dimensions={0} | all-to-all | bytes 163840 | tf_op jit(solution)/shard_map/all_to_all | solution.py:327
  170.0 8.6 %certain_run.3 = (f32[64,128]{1,0:T(8,128)}, f32[64,128]{1,0:T(8,128)}, f32[64,128]{1,0:T(8,128)}, f32[32,1,640]{2,1,0:T(1,128)}, f32[1,128]{1,0:T(1,128)}, /*index=5*/s32[1]{0:T(128)}) custom-call(f32[32,1,640]{2,1,0:T(1,128)} %all_to_all.55.refs_0_, f32[1,128]{1,0:T(1,128)} %get-tuple-element.74.refs_1_, s32[1]{0:T(128)} %get-tuple-element.75.refs_2_, ...), custom_call_target="tpu_custom_call" | custom-call | tf_op jit(solution)/shard_map/certain_run/pallas_call | solution.py:362
  178.6 13.8 %all_to_all.56.notes = f32[32,1,640]{2,1,0:T(1,128)} all-to-all(f32[32,1,640]{2,1,0:T(1,128)} %get-tuple-element.76), channel_id=1, replica_groups=mesh['z'=32,'core'=2,'col'=16] {'core','col'}, dimensions={0} | all-to-all | bytes 163840 | tf_op jit(solution)/shard_map/all_to_all | solution.py:326
  192.3 1.7 merge_notes.7
  194.0 30.4 %all_to_all.57.refs_0_ = f32[32,1,640]{2,1,0:T(1,128)} all-to-all(f32[32,1,640]{2,1,0:T(1,128)} %merge_notes.7), channel_id=1, replica_groups=mesh['z'=32,'core'=2,'col'=16] {'z'}, dimensions={0} | all-to-all | bytes 163840 | tf_op jit(solution)/shard_map/all_to_all | solution.py:327
  224.4 8.6 %later_run.2 = (f32[64,128]{1,0:T(8,128)}, f32[64,128]{1,0:T(8,128)}, f32[64,128]{1,0:T(8,128)}, f32[32,1,640]{2,1,0:T(1,128)}, f32[1,128]{1,0:T(1,128)S(1)}, /*index=5*/s32[1]{0:T(128)}) custom-call(f32[32,1,640]{2,1,0:T(1,128)} %all_to_all.57.refs_0_, f32[1,128]{1,0:T(1,128)} %get-tuple-element.77.refs_1_, s32[1]{0:T(128)} %get-tuple-element.78.refs_2_, ...), custom_call_target="tpu_custom_call" | custom-call | tf_op jit(solution)/shard_map/later_run/pallas_call | solution.py:362
  233.0 13.8 %all_to_all.58.notes = f32[32,1,640]{2,1,0:T(1,128)} all-to-all(f32[32,1,640]{2,1,0:T(1,128)} %get-tuple-element.79), channel_id=1, replica_groups=mesh['z'=32,'core'=2,'col'=16] {'core','col'}, dimensions={0} | all-to-all | bytes 163840 | tf_op jit(solution)/shard_map/all_to_all | solution.py:326
  246.8 1.7 merge_notes.8
  248.5 3.8 %all-to-all-start.9 = ((f32[32,1,640]{2,1,0:T(1,128)}), f32[32,1,640]{2,1,0:T(1,128)S(1)}, u32[]{:S(2)}, u32[]{:S(2)}) async-start(f32[32,1,640]{2,1,0:T(1,128)} %merge_notes.8), calls=%async_computation.9 | async-start | bytes 163840 | tf_op jit(solution)/shard_map/all_to_all | solution.py:327
  252.3 25.9 %all-to-all-done.9 = f32[32,1,640]{2,1,0:T(1,128)S(1)} async-done(((f32[32,1,640]{2,1,0:T(1,128)}), f32[32,1,640]{2,1,0:T(1,128)S(1)}, u32[]{:S(2)}, u32[]{:S(2)}) %all-to-all-start.9) | async-done | bytes 81952 | tf_op jit(solution)/shard_map/all_to_all | solution.py:327
  278.2 0.1 slice_reduce_fusion.1
  278.2 0.7 compare_reduce_fusion.1
  278.9 55.5 %while.22 = (s32[]{:T(128)}, pred[]{:T(512)}, f32[32,1,640]{2,1,0:T(1,128)S(1)}, f32[1,128]{1,0:T(1,128)S(1)}, s32[1]{0:T(128)}, /*index=5*/f32[64,128]{1,0:T(8,...) while((s32[]{:T(128)}, pred[]{:T(512)}, f32[32,1,640]{2,1,0:T(1,128)S(1)}, ...), condition=%wide.region_5.6_spmd, body=%wide.region_2.5_spmd.sunk | while | flops 399 | bytes 412451 | solution.py:375
  280.2 0.5 copy.42.refs_1_
  280.7 7.1 %later_run.3 = (f32[64,128]{1,0:T(8,128)}, f32[64,128]{1,0:T(8,128)}, f32[64,128]{1,0:T(8,128)}, f32[32,1,640]{2,1,0:T(1,128)}, f32[1,128]{1,0:T(1,128)S(1)}, /*index=5*/s32[1]{0:T(128)}) custom-call(f32[32,1,640]{2,1,0:T(1,128)S(1)} %get-tuple-element.190.refs_0_, f32[1,128]{1,0:T(1,128)} %copy.42.refs_1_, s32[1]{0:T(128)S(6)} %copy.43.refs_2_, ...), custom_call_target="tpu_custom_call" | custom-call | tf_op jit(solution)/shard_map/while/body/later_run/pallas_call | solution.py:370
  287.9 13.8 %all_to_all.59.notes = f32[32,1,640]{2,1,0:T(1,128)} all-to-all(f32[32,1,640]{2,1,0:T(1,128)} %get-tuple-element.172), channel_id=1, replica_groups=mesh['z'=32,'core'=2,'col'=16] {'core','col'}, dimensions={0} | all-to-all | bytes 163840 | tf_op jit(solution)/shard_map/while/body/all_to_all | solution.py:326
  301.6 1.7 merge_notes.9
  303.3 3.8 %all-to-all-start.1 = ((f32[32,1,640]{2,1,0:T(1,128)}), f32[32,1,640]{2,1,0:T(1,128)S(1)}, u32[]{:S(2)}, u32[]{:S(2)}) async-start(f32[32,1,640]{2,1,0:T(1,128)} %merge_notes.9), calls=%async_computation.1 | async-start | bytes 163840 | tf_op jit(solution)/shard_map/while/body/all_to_all | solution.py:327
  307.2 25.9 %all-to-all-done.1 = f32[32,1,640]{2,1,0:T(1,128)S(1)} async-done(((f32[32,1,640]{2,1,0:T(1,128)}), f32[32,1,640]{2,1,0:T(1,128)S(1)}, u32[]{:S(2)}, u32[]{:S(2)}) %all-to-all-start.1) | async-done | bytes 81952 | tf_op jit(solution)/shard_map/while/body/all_to_all | solution.py:327
  333.1 0.1 slice_reduce_fusion.3
  333.1 0.7 compare_reduce_fusion.3
  (9 shorter events, 0.1 us)
Async XLA Ops:
  0.6 11.6 %copy-start = (f32[64,128]{1,0:T(8,128)S(1)}, f32[64,128]{1,0:T(8,128)}, u32[]{:S(2)}) copy-start(f32[64,128]{1,0:T(8,128)} %param.9) | copy-start | bytes 98308
  12.2 0.8 copy-start.1
  13.0 0.8 copy-start.2
  13.8 0.8 copy-start.3
  14.5 0.8 copy-start.4
  15.3 0.8 copy-start.5
  16.1 18.0 %collective-permute-start = (f32[6,12,128]{2,1,0:T(8,128)S(1)}, f32[6,12,128]{2,1,0:T(8,128)S(1)}, u32[]{:S(2)}, u32[]{:S(2)}) collective-permute-start(f32[6,12,128]{2,1,0:T(8,128)S(1)} %get-tuple-element.108), channel_id=1, source_target_pairs={{16,0},{32,16},{48,32},{64,48},{80,64},{96,80},{112,96},{128,112},... | collective-permute-start | bytes 110600 | tf_op jit(solution)/shard_map/ppermute | solution.py:54
  32.1 3.1 collective-permute-start.1
  35.4 9.8 %collective-permute-start.2 = (f32[6,88,12]{2,1,0:T(8,128)S(1)}, f32[6,88,12]{2,1,0:T(8,128)S(1)}, u32[]{:S(2)}, u32[]{:S(2)}) collective-permute-start(f32[6,88,12]{2,1,0:T(8,128)S(1)} %get-tuple-element.106), channel_id=1, source_target_pairs={{1,0},{2,1},{3,2},{4,3},{5,4},{6,5},{7,6},{8,7},{9,8},{10,9},{11,1... | collective-permute-start | bytes 76040 | tf_op jit(solution)/shard_map/ppermute | solution.py:58
  36.7 9.4 %collective-permute-start.3 = (f32[6,88,12]{2,1,0:T(8,128)S(1)}, f32[6,88,12]{2,1,0:T(8,128)S(1)}, u32[]{:S(2)}, u32[]{:S(2)}) collective-permute-start(f32[6,88,12]{2,1,0:T(8,128)S(1)} %get-tuple-element.107), channel_id=1, source_target_pairs={{0,1},{1,2},{2,3},{3,4},{4,5},{5,6},{6,7},{7,8},{8,9},{9,10},{10,1... | collective-permute-start | bytes 76040 | tf_op jit(solution)/shard_map/ppermute | solution.py:57
  248.5 29.7 %all-to-all-start.9 = ((f32[32,1,640]{2,1,0:T(1,128)}), f32[32,1,640]{2,1,0:T(1,128)S(1)}, u32[]{:S(2)}, u32[]{:S(2)}) async-start(f32[32,1,640]{2,1,0:T(1,128)} %merge_notes.8), calls=%async_computation.9 | async-start | bytes 163840 | tf_op jit(solution)/shard_map/all_to_all | solution.py:327
  303.3 29.7 %all-to-all-start.1 = ((f32[32,1,640]{2,1,0:T(1,128)}), f32[32,1,640]{2,1,0:T(1,128)S(1)}, u32[]{:S(2)}, u32[]{:S(2)}) async-start(f32[32,1,640]{2,1,0:T(1,128)} %merge_notes.9), calls=%async_computation.1 | async-start | bytes 163840 | tf_op jit(solution)/shard_map/while/body/all_to_all | solution.py:327
where the time goes:
time: 336 us; the launch traced here: 334 us
  blocking collectives  178 us (53%)
  waiting for transfers between devices  58.2 us (17%)
  Pallas kernels  47.3 us (14%)
  starting transfers between devices  30.9 us (9%)
  between operations  10.8 us (3%)
  local copies, waits for them, and re-layouts  6.1 us (2%)
    all_to_all x3, blocking collectives, everywhere(): return lax.all_to_all(merge(over_plane), 'z', 0, 0, tiled=True)  109 us
    all_to_all x5, blocking collectives, everywhere(): over_plane = lax.all_to_all(note, plane, 0, 0, tiled=True)  68.3 us
    all_to_all x2, waiting for transfers between devices, everywhere(): return lax.all_to_all(merge(over_plane), 'z', 0, 0, tiled=True)  51.8 us
    pallas_call x3, Pallas kernels, per_device(): *result, note, guess, known = again(everywhere(note), guess, known, fields)  25.8 us
    ppermute x1, starting transfers between devices, with_halo(): after = lax.ppermute(fields[:, :HALO], ROW, down)  16 us
    pallas_call x5, Pallas kernels, everywhere(): return lax.all_to_all(merge(over_plane), 'z', 0, 0, tiled=True)  8.45 us
    all_to_all x2, starting transfers between devices, everywhere(): return lax.all_to_all(merge(over_plane), 'z', 0, 0, tiled=True)  7.68 us
    pallas_call x1, Pallas kernels, one_round(): *result, note, guess, known = later(notes, guess, known, fields)  7.14 us
  transfers between devices with their start and end apart: 6, of which 5 were waited for; matrix products, arithmetic and copies ran while one was open for 0% of the time, Pallas kernels for 0%

commit v1 on v0

--- a/solution.py
+++ b/solution.py
@@ -47,17 +47,58 @@
     return up, down
 
 
-def with_halo(fields):
+def prepare_kernel(table, depth, elevation, flow_x, flow_y, wet, classes, fields, first, last, whole, sems):
+    places = (
+        (depth, fields.at[0]),
+        (flow_x, fields.at[1]),
+        (flow_y, fields.at[2]),
+        (elevation, fields.at[3]),
+        (classes, whole.at[0]),
+        (wet, whole.at[1]),
+    )
+    copies = [pltpu.make_async_copy(src, dst, sems.at[i]) for i, (src, dst) in enumerate(places)]
+    for copy in copies:
+        copy.start()
+    for copy in copies:
+        copy.wait()
+    class_of = whole[0]
+    rough_sq = jnp.zeros(class_of.shape, jnp.float32)
+    for class_id in range(CLASSES):
+        rough_sq = rough_sq + jnp.where(class_of == class_id, table[class_id] * table[class_id], 0.0)
+    fields[4] = rough_sq
+    fields[5] = whole[1].astype(jnp.float32)
+    rows = class_of.shape[0]
+    for f in range(FIELDS):
+        first[f] = fields[f, :HALO]
+        last[f] = fields[f, rows - HALO :]
+
+
+def edge_kernel(fields, after, before, tall, first, last):
     rows, cols = fields.shape[1:]
-    up, down = neighbours(ROW)
-    before = lax.ppermute(fields[:, rows - HALO :], ROW, up)
-    after = lax.ppermute(fields[:, :HALO], ROW, down)
-    fields = jnp.concatenate([fields, after, before], axis=1)
-    up, down = neighbours("col")
-    before = lax.ppermute(fields[:, :, cols - HALO :], "col", up)
-    after = lax.ppermute(fields[:, :, :HALO], "col", down)
-    gap = jnp.zeros((*fields.shape[:2], cols - 2 * HALO), fields.dtype)
-    return jnp.concatenate([fields, after, gap, before], axis=2)
+    shape = first.shape
+    lane = lanes_of(shape)
+    packed = [jnp.zeros(shape, jnp.float32)] * 2
+    for f in range(FIELDS):
+        tall[f, :rows] = fields[f]
+        tall[f, rows : rows + HALO] = after[f]
+        tall[f, rows + HALO :] = before[f]
+        here = (lane >= HALO * f) & (lane < HALO * (f + 1))
+        whole = tall[f]
+        for end, start in enumerate((0, cols - HALO)):
+            packed[end] = jnp.where(here, turned(whole, HALO * f - start, 1), packed[end])
+    first[...] = packed[0]
+    last[...] = packed[1]
+
+
+def join(fields, tall, after, before):
+    cols = tall.shape[2]
+    lane = lanes_of(after.shape)
+    ahead, behind = after[...], before[...]
+    for f in range(FIELDS):
+        fields[f, :, :cols] = tall[f]
+        rest = jnp.where(lane < HALO, turned(ahead, -HALO * f, 1), 0.0)
+        rest = jnp.where(lane >= cols - HALO, turned(behind, cols - HALO - HALO * f, 1), rest)
+        fields[f, :, cols:] = rest
 
 
 def next_of(x, axis):
@@ -192,7 +233,8 @@
 
 def run_kernel(tile, first, certain, *refs):
     if first:
-        fields, depth_out, flow_x_out, flow_y_out, note_out, guess_out, known_out = refs[:7]
+        tall, after, before, fields, depth_out, flow_x_out, flow_y_out, note_out, guess_out, known_out = refs[:10]
+        join(fields, tall, after, before)
     else:
         notes, guess_in, known_in, fields, depth_out, flow_x_out, flow_y_out, note_out, guess_out, known_out = refs[:10]
     state, faces, saved, guesses, depths, spots = refs[-6:]
@@ -305,20 +347,36 @@
 
 
 def per_device(depth, elevation, flow_x, flow_y, wet_mask, manning_class, manning_table):
-    rough_sq = jnp.zeros(depth.shape, jnp.float32)
-    for class_id in range(CLASSES):
-        rough_sq = rough_sq + jnp.where(
-            manning_class == class_id, manning_table[class_id] * manning_table[class_id], 0.0
-        )
-    wet_open = wet_mask.astype(jnp.float32)
     tile = depth.shape
     plane = ("core", "col")
     near_peers, far_peers = lax.axis_size("core") * lax.axis_size("col"), lax.axis_size("z")
-    fields = with_halo(jnp.stack([depth, flow_x, flow_y, elevation, rough_sq, wet_open]))
-    large = fields.shape[1:]
+    rows, cols = tile
+    large = (rows + 2 * HALO, 2 * cols)
+    vmem = pl.BlockSpec(memory_space=pltpu.VMEM)
+    smem = pl.BlockSpec(memory_space=pltpu.SMEM)
 
     def f32(*shape):
         return jax.ShapeDtypeStruct(shape, jnp.float32)
+
+    fields, first, last = pl.pallas_call(
+        prepare_kernel,
+        in_specs=[smem] + [pl.BlockSpec(memory_space=pl.ANY)] * 6,
+        out_shape=(f32(FIELDS, *tile), f32(FIELDS, HALO, cols), f32(FIELDS, HALO, cols)),
+        out_specs=(vmem,) * 3,
+        scratch_shapes=[pltpu.VMEM((2, *tile), jnp.int32), pltpu.SemaphoreType.DMA((6,))],
+        name="prepare",
+    )(manning_table, depth, elevation, flow_x, flow_y, wet_mask, manning_class)
+    up, down = neighbours(ROW)
+    before, after = lax.ppermute(last, ROW, up), lax.ppermute(first, ROW, down)
+    tall, first, last = pl.pallas_call(
+        edge_kernel,
+        in_specs=[vmem] * 3,
+        out_shape=(f32(FIELDS, large[0], cols), f32(large[0], 128), f32(large[0], 128)),
+        out_specs=(vmem,) * 3,
+        name="edges",
+    )(fields, after, before)
+    up, down = neighbours("col")
+    before, after = lax.ppermute(last, "col", up), lax.ppermute(first, "col", down)
 
     merge = pl.pallas_call(merge_kernel, out_shape=f32(far_peers, 1, NOTE), name="merge_notes")
 
@@ -327,12 +385,12 @@
         return lax.all_to_all(merge(over_plane), "z", 0, 0, tiled=True)
 
     def run(first, certain=False):
-        vmem = pl.BlockSpec(memory_space=pltpu.VMEM)
-        smem = pl.BlockSpec(memory_space=pltpu.SMEM)
+        whole = (f32(FIELDS, *large),) if first else ()
         return pl.pallas_call(
             lambda *refs: run_kernel(tile, first, certain, *refs),
-            in_specs=[vmem] if first else [vmem, vmem, smem, vmem],
+            in_specs=[vmem] * 3 if first else [vmem, vmem, smem, vmem],
             out_shape=(
+                *whole,
                 f32(*tile),
                 f32(*tile),
                 f32(*tile),
@@ -340,7 +398,7 @@
                 f32(1, 128),
                 jax.ShapeDtypeStruct((1,), jnp.int32),
             ),
-            out_specs=(vmem, vmem, vmem, vmem, vmem, smem),
+            out_specs=(vmem,) * (5 + len(whole)) + (smem,),
             scratch_shapes=[
                 pltpu.VMEM((3, *large), jnp.float32),
                 pltpu.VMEM((4, *large), jnp.float32),
@@ -356,7 +414,7 @@
         true = jnp.max(notes[:, 0, :ITERS], axis=0)
         return jnp.all(true == guess[0, :ITERS])
 
-    *result, note, guess, known = run(True)(fields)
+    fields, *result, note, guess, known = run(True)(tall, after, before)
     certain, later = run(False, True), run(False)
     for again in (certain, certain, later):
         *result, note, guess, known = again(everywhere(note), guess, known, fields)

time: 336 us -> 325 us (0.967)
  between operations: 10.8 us -> 0.76 us
  Pallas kernels: 47.3 us -> 52.4 us
  local copies, waits for them, and re-layouts: 6.1 us -> 1.75 us
  waiting for transfers between devices: 58.2 us -> 54.6 us
    pallas_call x1 -> x3, Pallas kernels: 5.84 us -> 11.1 us  [the longest x1 6.98 us: per_device(): fields, *result, note, guess, known = run(True)(tall, after, before)]
    ppermute x4, waiting for transfers between devices: 6.46 us -> 2.87 us  [the longest x1 1.45 us: per_device(): lax.ppermute(last, ROW, up)]
  transfers between devices with their start and end apart: 6 -> 6, of which waited for: 5 -> 4; matrix products, arithmetic and copies ran while one was open for 0% -> 0% of each run, Pallas kernels for 0% -> 0%
where the time goes in v1:
time: 325 us; the launch traced here: 323 us
  blocking collectives  179 us (55%)
  waiting for transfers between devices  54.6 us (17%)
  Pallas kernels  52.4 us (16%)
  starting transfers between devices  30.9 us (10%)
    all_to_all x3, blocking collectives, everywhere(): return lax.all_to_all(merge(over_plane), 'z', 0, 0, tiled=True)  111 us
    all_to_all x5, blocking collectives, everywhere(): over_plane = lax.all_to_all(note, plane, 0, 0, tiled=True)  68.3 us
    all_to_all x2, waiting for transfers between devices, everywhere(): return lax.all_to_all(merge(over_plane), 'z', 0, 0, tiled=True)  51.8 us
    pallas_call x3, Pallas kernels, per_device(): *result, note, guess, known = again(everywhere(note), guess, known, fields)  25.8 us
    ppermute x1, starting transfers between devices, per_device(): lax.ppermute(first, ROW, down)  16 us
    pallas_call x5, Pallas kernels, everywhere(): return lax.all_to_all(merge(over_plane), 'z', 0, 0, tiled=True)  8.39 us
    all_to_all x2, starting transfers between devices, everywhere(): return lax.all_to_all(merge(over_plane), 'z', 0, 0, tiled=True)  7.7 us
    pallas_call x1, Pallas kernels, one_round(): *result, note, guess, known = later(notes, guess, known, fields)  7.12 us
  transfers between devices with their start and end apart: 6, of which 4 were waited for; matrix products, arithmetic and copies ran while one was open for 0% of the time, Pallas kernels for 0%

profile of v1, /device:TPU:1, one launch (start us, length us, event | category | flops | bytes accessed | tf_op | source)
XLA Modules:
  0.0 323.3 jit_solution(4976702062741831127)
XLA Ops:
  0.6 2.3 prepare.1
  2.9 16.0 %collective-permute-start = (f32[6,12,128]{2,1,0:T(8,128)}, f32[6,12,128]{2,1,0:T(8,128)S(1)}, u32[]{:S(2)}, u32[]{:S(2)}) collective-permute-start(f32[6,12,128]{2,1,0:T(8,128)} %get-tuple-element.78), channel_id=1, source_target_pairs={{16,0},{32,16},{48,32},{64,48},{80,64},{96,80},{112,96},{128,112},... | collective-permute-start | bytes 110600 | tf_op jit(solution)/shard_map/ppermute | solution.py:370
  19.0 1.9 collective-permute-start.1
  20.9 0.0 collective-permute-done.after
  20.9 0.0 copy-start
  20.9 1.5 collective-permute-done.1.before
  22.4 0.0 copy-start.1
  22.4 0.0 copy-done
  22.4 0.6 copy-done.1
  23.0 1.8 edges.1
  24.8 1.3 collective-permute-start.2
  26.0 4.0 %collective-permute-start.3 = (f32[88,128]{1,0:T(8,128)}, f32[88,128]{1,0:T(8,128)S(1)}, u32[]{:S(2)}, u32[]{:S(2)}) collective-permute-start(f32[88,128]{1,0:T(8,128)} %get-tuple-element.82), channel_id=1, source_target_pairs={{0,1},{1,2},{2,3},{3,4},{4,5},{5,6},{6,7},{7,8},{8,9},{9,10},{10,1... | collective-permute-start | bytes 135176 | tf_op jit(solution)/shard_map/ppermute | solution.py:379
  30.0 0.0 collective-permute-done.2.refs_1_
  30.1 0.0 copy-start.2
  30.1 1.4 collective-permute-done.3.refs_2_
  31.5 0.0 copy-start.3
  31.5 0.0 copy-done.2
  31.5 0.6 copy-done.3
  32.1 7.0 %first_run.1 = (f32[6,88,256]{2,1,0:T(8,128)S(1)}, f32[64,128]{1,0:T(8,128)}, f32[64,128]{1,0:T(8,128)}, f32[64,128]{1,0:T(8,128)}, f32[32,1,640]{2,1,0:T(1,128)}, /*index=5*/f32[1,128]{1,0:T(1,128)}, s32[1]{0:T(128)}) custom-call(f32[6,88,128]{2,1,0:T(8,128)} %get-tuple-element.80.refs_0_, f32[88,128]{1,0:T(8,128)} %copy-done.2, f32[88,128]{1,0:T(8,128)} %copy-done.3), custom_call_target="tpu_custom_call" | custom-call | tf_op jit(solution)/shard_map/first_run/pallas_call | solution.py:417
  39.1 12.7 %all_to_all.52.notes = f32[32,1,640]{2,1,0:T(1,128)} all-to-all(f32[32,1,640]{2,1,0:T(1,128)} %get-tuple-element.83), channel_id=1, replica_groups=mesh['z'=32,'core'=2,'col'=16] {'core','col'}, dimensions={0} | all-to-all | bytes 163840 | tf_op jit(solution)/shard_map/all_to_all | solution.py:384
  51.8 1.7 merge_notes.5
  53.4 50.2 %all_to_all.53.refs_0_ = f32[32,1,640]{2,1,0:T(1,128)} all-to-all(f32[32,1,640]{2,1,0:T(1,128)} %merge_notes.5), channel_id=1, replica_groups=mesh['z'=32,'core'=2,'col'=16] {'z'}, dimensions={0} | all-to-all | bytes 163840 | tf_op jit(solution)/shard_map/all_to_all | solution.py:385
  103.7 8.6 %certain_run.2 = (f32[64,128]{1,0:T(8,128)}, f32[64,128]{1,0:T(8,128)}, f32[64,128]{1,0:T(8,128)}, f32[32,1,640]{2,1,0:T(1,128)}, f32[1,128]{1,0:T(1,128)}, /*index=5*/s32[1]{0:T(128)}) custom-call(f32[32,1,640]{2,1,0:T(1,128)} %all_to_all.53.refs_0_, f32[1,128]{1,0:T(1,128)} %get-tuple-element.84.refs_1_, s32[1]{0:T(128)} %get-tuple-element.85.refs_2_, ...), custom_call_target="tpu_custom_call" | custom-call | tf_op jit(solution)/shard_map/certain_run/pallas_call | solution.py:420
  112.3 14.2 %all_to_all.54.notes = f32[32,1,640]{2,1,0:T(1,128)} all-to-all(f32[32,1,640]{2,1,0:T(1,128)} %get-tuple-element.87), channel_id=1, replica_groups=mesh['z'=32,'core'=2,'col'=16] {'core','col'}, dimensions={0} | all-to-all | bytes 163840 | tf_op jit(solution)/shard_map/all_to_all | solution.py:384
  126.6 1.7 merge_notes.6
  128.2 30.4 %all_to_all.55.refs_0_ = f32[32,1,640]{2,1,0:T(1,128)} all-to-all(f32[32,1,640]{2,1,0:T(1,128)} %merge_notes.6), channel_id=1, replica_groups=mesh['z'=32,'core'=2,'col'=16] {'z'}, dimensions={0} | all-to-all | bytes 163840 | tf_op jit(solution)/shard_map/all_to_all | solution.py:385
  158.7 8.6 %certain_run.3 = (f32[64,128]{1,0:T(8,128)}, f32[64,128]{1,0:T(8,128)}, f32[64,128]{1,0:T(8,128)}, f32[32,1,640]{2,1,0:T(1,128)}, f32[1,128]{1,0:T(1,128)}, /*index=5*/s32[1]{0:T(128)}) custom-call(f32[32,1,640]{2,1,0:T(1,128)} %all_to_all.55.refs_0_, f32[1,128]{1,0:T(1,128)} %get-tuple-element.88.refs_1_, s32[1]{0:T(128)} %get-tuple-element.89.refs_2_, ...), custom_call_target="tpu_custom_call" | custom-call | tf_op jit(solution)/shard_map/certain_run/pallas_call | solution.py:420
  167.3 13.8 %all_to_all.56.notes = f32[32,1,640]{2,1,0:T(1,128)} all-to-all(f32[32,1,640]{2,1,0:T(1,128)} %get-tuple-element.90), channel_id=1, replica_groups=mesh['z'=32,'core'=2,'col'=16] {'core','col'}, dimensions={0} | all-to-all | bytes 163840 | tf_op jit(solution)/shard_map/all_to_all | solution.py:384
  181.1 1.7 merge_notes.7
  182.8 30.4 %all_to_all.57.refs_0_ = f32[32,1,640]{2,1,0:T(1,128)} all-to-all(f32[32,1,640]{2,1,0:T(1,128)} %merge_notes.7), channel_id=1, replica_groups=mesh['z'=32,'core'=2,'col'=16] {'z'}, dimensions={0} | all-to-all | bytes 163840 | tf_op jit(solution)/shard_map/all_to_all | solution.py:385
  213.2 8.6 %later_run.2 = (f32[64,128]{1,0:T(8,128)}, f32[64,128]{1,0:T(8,128)}, f32[64,128]{1,0:T(8,128)}, f32[32,1,640]{2,1,0:T(1,128)}, f32[1,128]{1,0:T(1,128)S(1)}, /*index=5*/s32[1]{0:T(128)}) custom-call(f32[32,1,640]{2,1,0:T(1,128)} %all_to_all.57.refs_0_, f32[1,128]{1,0:T(1,128)} %get-tuple-element.91.refs_1_, s32[1]{0:T(128)} %get-tuple-element.92.refs_2_, ...), custom_call_target="tpu_custom_call" | custom-call | tf_op jit(solution)/shard_map/later_run/pallas_call | solution.py:420
  221.8 13.8 %all_to_all.58.notes = f32[32,1,640]{2,1,0:T(1,128)} all-to-all(f32[32,1,640]{2,1,0:T(1,128)} %get-tuple-element.93), channel_id=1, replica_groups=mesh['z'=32,'core'=2,'col'=16] {'core','col'}, dimensions={0} | all-to-all | bytes 163840 | tf_op jit(solution)/shard_map/all_to_all | solution.py:384
  235.6 1.7 merge_notes.8
  237.2 3.8 %all-to-all-start.9 = ((f32[32,1,640]{2,1,0:T(1,128)}), f32[32,1,640]{2,1,0:T(1,128)S(1)}, u32[]{:S(2)}, u32[]{:S(2)}) async-start(f32[32,1,640]{2,1,0:T(1,128)} %merge_notes.8), calls=%async_computation.9 | async-start | bytes 163840 | tf_op jit(solution)/shard_map/all_to_all | solution.py:385
  241.1 25.9 %all-to-all-done.9 = f32[32,1,640]{2,1,0:T(1,128)S(1)} async-done(((f32[32,1,640]{2,1,0:T(1,128)}), f32[32,1,640]{2,1,0:T(1,128)S(1)}, u32[]{:S(2)}, u32[]{:S(2)}) %all-to-all-start.9) | async-done | bytes 81952 | tf_op jit(solution)/shard_map/all_to_all | solution.py:385
  267.0 0.1 slice_reduce_fusion.1
  267.0 0.7 compare_reduce_fusion.1
  267.7 55.6 %while.22 = (s32[]{:T(128)}, pred[]{:T(512)}, f32[32,1,640]{2,1,0:T(1,128)S(1)}, f32[1,128]{1,0:T(1,128)S(1)}, s32[1]{0:T(128)}, /*index=5*/f32[64,128]{1,0:T(8,...) while((s32[]{:T(128)}, pred[]{:T(512)}, f32[32,1,640]{2,1,0:T(1,128)S(1)}, ...), condition=%wide.region_5.0_spmd, body=%wide.region_2.0_spmd.sunk | while | flops 399 | bytes 412451 | solution.py:433
  269.0 0.5 copy.37.refs_1_
  269.5 7.1 %later_run.3 = (f32[64,128]{1,0:T(8,128)}, f32[64,128]{1,0:T(8,128)}, f32[64,128]{1,0:T(8,128)}, f32[32,1,640]{2,1,0:T(1,128)}, f32[1,128]{1,0:T(1,128)S(1)}, /*index=5*/s32[1]{0:T(128)}) custom-call(f32[32,1,640]{2,1,0:T(1,128)S(1)} %get-tuple-element.192.refs_0_, f32[1,128]{1,0:T(1,128)} %copy.37.refs_1_, s32[1]{0:T(128)S(6)} %copy.38.refs_2_, ...), custom_call_target="tpu_custom_call" | custom-call | tf_op jit(solution)/shard_map/while/body/later_run/pallas_call | solution.py:428
  276.7 13.8 %all_to_all.59.notes = f32[32,1,640]{2,1,0:T(1,128)} all-to-all(f32[32,1,640]{2,1,0:T(1,128)} %get-tuple-element.174), channel_id=1, replica_groups=mesh['z'=32,'core'=2,'col'=16] {'core','col'}, dimensions={0} | all-to-all | bytes 163840 | tf_op jit(solution)/shard_map/while/body/all_to_all | solution.py:384
  290.5 1.7 merge_notes.9
  292.2 3.9 %all-to-all-start.1 = ((f32[32,1,640]{2,1,0:T(1,128)}), f32[32,1,640]{2,1,0:T(1,128)S(1)}, u32[]{:S(2)}, u32[]{:S(2)}) async-start(f32[32,1,640]{2,1,0:T(1,128)} %merge_notes.9), calls=%async_computation.1 | async-start | bytes 163840 | tf_op jit(solution)/shard_map/while/body/all_to_all | solution.py:385
  296.0 25.9 %all-to-all-done.1 = f32[32,1,640]{2,1,0:T(1,128)S(1)} async-done(((f32[32,1,640]{2,1,0:T(1,128)}), f32[32,1,640]{2,1,0:T(1,128)S(1)}, u32[]{:S(2)}, u32[]{:S(2)}) %all-to-all-start.1) | async-done | bytes 81952 | tf_op jit(solution)/shard_map/while/body/all_to_all | solution.py:385
  321.9 0.1 slice_reduce_fusion.3
  322.0 0.7 compare_reduce_fusion.3
Async XLA Ops:
  2.9 18.0 %collective-permute-start = (f32[6,12,128]{2,1,0:T(8,128)}, f32[6,12,128]{2,1,0:T(8,128)S(1)}, u32[]{:S(2)}, u32[]{:S(2)}) collective-permute-start(f32[6,12,128]{2,1,0:T(8,128)} %get-tuple-element.78), channel_id=1, source_target_pairs={{16,0},{32,16},{48,32},{64,48},{80,64},{96,80},{112,96},{128,112},... | collective-permute-start | bytes 110600 | tf_op jit(solution)/shard_map/ppermute | solution.py:370
  19.0 3.4 %collective-permute-start.1 = (f32[6,12,128]{2,1,0:T(8,128)}, f32[6,12,128]{2,1,0:T(8,128)S(1)}, u32[]{:S(2)}, u32[]{:S(2)}) collective-permute-start(f32[6,12,128]{2,1,0:T(8,128)} %get-tuple-element.79), channel_id=1, source_target_pairs={{0,16},{16,32},{32,48},{48,64},{64,80},{80,96},{96,112},{112,128},... | collective-permute-start | bytes 110600 | tf_op jit(solution)/shard_map/ppermute | solution.py:370
  20.9 1.5 copy-start
  22.4 0.6 copy-start.1
  24.8 5.3 %collective-permute-start.2 = (f32[88,128]{1,0:T(8,128)}, f32[88,128]{1,0:T(8,128)S(1)}, u32[]{:S(2)}, u32[]{:S(2)}) collective-permute-start(f32[88,128]{1,0:T(8,128)} %get-tuple-element.81), channel_id=1, source_target_pairs={{1,0},{2,1},{3,2},{4,3},{5,4},{6,5},{7,6},{8,7},{9,8},{10,9},{11,1... | collective-permute-start | bytes 135176 | tf_op jit(solution)/shard_map/ppermute | solution.py:379
  26.0 5.4 %collective-permute-start.3 = (f32[88,128]{1,0:T(8,128)}, f32[88,128]{1,0:T(8,128)S(1)}, u32[]{:S(2)}, u32[]{:S(2)}) collective-permute-start(f32[88,128]{1,0:T(8,128)} %get-tuple-element.82), channel_id=1, source_target_pairs={{0,1},{1,2},{2,3},{3,4},{4,5},{5,6},{6,7},{7,8},{8,9},{9,10},{10,1... | collective-permute-start | bytes 135176 | tf_op jit(solution)/shard_map/ppermute | solution.py:379
  30.1 1.4 copy-start.2
  31.5 0.6 copy-start.3
  237.2 29.7 %all-to-all-start.9 = ((f32[32,1,640]{2,1,0:T(1,128)}), f32[32,1,640]{2,1,0:T(1,128)S(1)}, u32[]{:S(2)}, u32[]{:S(2)}) async-start(f32[32,1,640]{2,1,0:T(1,128)} %merge_notes.8), calls=%async_computation.9 | async-start | bytes 163840 | tf_op jit(solution)/shard_map/all_to_all | solution.py:385
  292.2 29.7 %all-to-all-start.1 = ((f32[32,1,640]{2,1,0:T(1,128)}), f32[32,1,640]{2,1,0:T(1,128)S(1)}, u32[]{:S(2)}, u32[]{:S(2)}) async-start(f32[32,1,640]{2,1,0:T(1,128)} %merge_notes.9), calls=%async_computation.1 | async-start | bytes 163840 | tf_op jit(solution)/shard_map/while/body/all_to_all | solution.py:385

commit v2 on v1

--- a/solution.py
+++ b/solution.py
@@ -38,6 +38,8 @@
 
 PLACES, TILES = note_places()
 NOTE = 128 * TILES
+BRIEF = 128
+UNUSED = 1000
 
 
 def neighbours(axis):
@@ -153,6 +155,8 @@
 
 
 def merged(notes):
+    if notes.shape[1] == BRIEF:
+        return jnp.max(notes, axis=0, keepdims=True)
     head = notes[:, :128]
     lane = lanes_of(head.shape)
     out_lane = lanes_of((1, NOTE))
@@ -231,7 +235,7 @@
     return [folded[i : i + 1] for i in range(window + 1)]
 
 
-def run_kernel(tile, first, certain, *refs):
+def run_kernel(tile, first, certain, reads, writes, *refs):
     if first:
         tall, after, before, fields, depth_out, flow_x_out, flow_y_out, note_out, guess_out, known_out = refs[:10]
         join(fields, tall, after, before)
@@ -253,29 +257,30 @@
         before = known_in[0]
         held = miss > before
         guess = true
-        windows = {w: window_fields(note, w) for w in range(1, REACH + 1)}
-        walls = {w: fixed_parts(parts[3], parts[5]) for w, parts in windows.items()}
-        moving = {w: parts[:3] for w, parts in windows.items()}
-        for stage in range(1, REACH + 1):
-            level = jnp.max(jnp.where(line_lane == before + stage, guess, 0.0), axis=1, keepdims=True)
-            time_step = step_of(level)
-            for w in range(stage, REACH + 1):
-                moving[w] = advance(*moving[w], windows[w][3], windows[w][4], walls[w], time_step)
-            shape = window_shape(stage)
-            here = (rows_of(shape) == stage) & (lanes_of(shape) == stage)
-            centre = total(jnp.where(here, moving[stage][0], 0.0), jnp.max)
-            target = before + stage + 1
-            use = held & (target > miss) & (line_lane == target) & (centre > 0.0)
-            guess = jnp.where(use, centre, guess)
+        if reads:
+            windows = {w: window_fields(note, w) for w in range(1, REACH + 1)}
+            walls = {w: fixed_parts(parts[3], parts[5]) for w, parts in windows.items()}
+            moving = {w: parts[:3] for w, parts in windows.items()}
+            for stage in range(1, REACH + 1):
+                level = jnp.max(jnp.where(line_lane == before + stage, guess, 0.0), axis=1, keepdims=True)
+                time_step = step_of(level)
+                for w in range(stage, REACH + 1):
+                    moving[w] = advance(*moving[w], windows[w][3], windows[w][4], walls[w], time_step)
+                shape = window_shape(stage)
+                here = (rows_of(shape) == stage) & (lanes_of(shape) == stage)
+                centre = total(jnp.where(here, moving[stage][0], 0.0), jnp.max)
+                target = before + stage + 1
+                use = held & (target > miss) & (line_lane == target) & (centre > 0.0)
+                guess = jnp.where(use, centre, guess)
         known = miss
-        if not certain:
+        if reads and not certain:
             known = jnp.where(held, jnp.maximum(before + REACH + 1, miss), miss)
         guess_out[...] = guess
         square = (16, 128)
         onto = rows_of(square) == lanes_of(square)
         spread = jnp.sum(jnp.where(onto, jnp.broadcast_to(guess, square), 0.0), axis=1, keepdims=True)
         guesses[...] = jnp.broadcast_to(spread, square)
-    known_out[0] = known
+    known_out[0] = known if writes or first else jnp.int32(UNUSED)
 
     for f in range(3):
         state[f] = fields[f]
@@ -284,9 +289,10 @@
         faces[2 * axis] = bed_max
         faces[2 * axis + 1] = both
     last = fields.shape[1] - 8
-    for f in range(3, FIELDS):
-        saved[f, :8] = fields[f, last:]
-        saved[f, 8:] = fields[f]
+    if writes:
+        for f in range(3, FIELDS):
+            saved[f, :8] = fields[f, last:]
+            saved[f, 8:] = fields[f]
     depths[...] = jnp.full(depths.shape, -1.0, jnp.float32)
 
     def one_step(step, carry):
@@ -295,13 +301,13 @@
         deepest = total(own, jnp.max)
         depths[pl.ds(step, 1), :] = jnp.broadcast_to(deepest, (1, 128))
 
-        @pl.when(step == known + 1)
+        @pl.when((step == known + 1) & writes)
         def _():
             for f in range(3):
                 saved[f, :8] = state[f, last:]
                 saved[f, 8:] = state[f]
 
-        for j in range(REACH):
+        for j in range(REACH if writes else 0):
 
             @pl.when(step == known + 2 + j)
             def _():
@@ -332,8 +338,8 @@
     square = depths.shape
     onto = rows_of(square) == lanes_of(square)
     low = jnp.sum(jnp.where(onto, depths[...], 0.0), axis=0, keepdims=True)
-    note = [low] + [jnp.zeros((1, 128), jnp.float32)] * (TILES - 1)
-    for j in range(REACH):
+    note = [low] + [jnp.zeros((1, 128), jnp.float32)] * (TILES - 1 if writes else 0)
+    for j in range(REACH if writes else 0):
         window = j + 1
         key = jnp.max(jnp.where(line_lane == known + 1 + window, low, -1.0), axis=1, keepdims=True)
         note[0] = jnp.where(line_lane == KEYS + j, key, note[0])
@@ -342,7 +348,7 @@
             tile, at = PLACES[window, i]
             here = (line_lane >= at) & (line_lane < at + FIELDS * (2 * window + 1))
             note[tile] = jnp.where(here, turned(line, at, 1), note[tile])
-    note = jnp.concatenate(note, axis=1)
+    note = jnp.concatenate(note, axis=1) if writes else low
     note_out[...] = jnp.broadcast_to(note[:, None, :], note_out.shape)
 
 
@@ -378,23 +384,23 @@
     up, down = neighbours("col")
     before, after = lax.ppermute(last, "col", up), lax.ppermute(first, "col", down)
 
-    merge = pl.pallas_call(merge_kernel, out_shape=f32(far_peers, 1, NOTE), name="merge_notes")
-
     def everywhere(note):
         over_plane = lax.all_to_all(note, plane, 0, 0, tiled=True)
+        merge = pl.pallas_call(merge_kernel, out_shape=f32(far_peers, 1, note.shape[2]), name="merge_notes")
         return lax.all_to_all(merge(over_plane), "z", 0, 0, tiled=True)
 
-    def run(first, certain=False):
+    def run(name, certain=False, reads=True, writes=True):
+        first = name == "first_run"
         whole = (f32(FIELDS, *large),) if first else ()
         return pl.pallas_call(
-            lambda *refs: run_kernel(tile, first, certain, *refs),
+            lambda *refs: run_kernel(tile, first, certain, reads, writes, *refs),
             in_specs=[vmem] * 3 if first else [vmem, vmem, smem, vmem],
             out_shape=(
                 *whole,
                 f32(*tile),
                 f32(*tile),
                 f32(*tile),
-                f32(near_peers, 1, NOTE),
+                f32(near_peers, 1, NOTE if writes else BRIEF),
                 f32(1, 128),
                 jax.ShapeDtypeStruct((1,), jnp.int32),
             ),
@@ -407,18 +413,25 @@
                 pltpu.VMEM((16, 128), jnp.float32),
                 pltpu.SMEM((REACH,), jnp.int32),
             ],
-            name="first_run" if first else "certain_run" if certain else "later_run",
+            name=name,
         )
 
     def settled(notes, guess):
         true = jnp.max(notes[:, 0, :ITERS], axis=0)
         return jnp.all(true == guess[0, :ITERS])
 
-    fields, *result, note, guess, known = run(True)(tall, after, before)
-    certain, later = run(False, True), run(False)
-    for again in (certain, certain, later):
+    fields, *result, note, guess, known = run("first_run", reads=False, writes=False)(tall, after, before)
+    later = run("later_run")
+    for again in (
+        run("second_run", certain=True, reads=False),
+        run("third_run", certain=True),
+        later,
+        run("check_run", writes=False),
+    ):
         *result, note, guess, known = again(everywhere(note), guess, known, fields)
     notes = everywhere(note)
+    done = settled(notes, guess)
+    notes = jnp.pad(notes, ((0, 0), (0, 0), (0, NOTE - BRIEF)))
 
     def unsettled(carry):
         return jnp.logical_not(carry[1]) & (carry[0] <= ITERS)
@@ -429,7 +442,7 @@
         notes = everywhere(note)
         return count + 1, settled(notes, guess), notes, guess, known, tuple(result)
 
-    carry = (jnp.int32(0), settled(notes, guess), notes, guess, known, tuple(result))
+    carry = (jnp.int32(0), done, notes, guess, known, tuple(result))
     return lax.while_loop(unsettled, one_round, carry)[-1]
 
 

time: 325 us -> 307 us (0.945)
  waiting for transfers between devices: 54.6 us -> 24 us
  blocking collectives: 179 us -> 204 us
  Pallas kernels: 52.4 us -> 47.7 us
  starting transfers between devices: 30.9 us -> 27 us
    all_to_all x2 -> x1, waiting for transfers between devices: 51.8 us -> 21.1 us  [everywhere(): return lax.all_to_all(merge(over_plane), 'z', 0, 0, tiled=True)]
    all_to_all x3 -> x4, blocking collectives: 111 us -> 137 us  [everywhere(): return lax.all_to_all(merge(over_plane), 'z', 0, 0, tiled=True)]
    pallas_call x2 -> x1, Pallas kernels: 14.1 us -> 5.04 us  [per_device(): run('first_run', reads=False, writes=False)(tall, after, before)]
    pallas_call x3 -> x4, Pallas kernels: 25.8 us -> 30.9 us  [per_device(): *result, note, guess, known = again(everywhere(note), guess, known, fields)]
    all_to_all x2 -> x1, starting transfers between devices: 7.7 us -> 3.79 us  [everywhere(): return lax.all_to_all(merge(over_plane), 'z', 0, 0, tiled=True)]
  transfers between devices with their start and end apart: 6 -> 5, of which waited for: 4 -> 3; matrix products, arithmetic and copies ran while one was open for 0% -> 0% of each run, Pallas kernels for 0% -> 0%
where the time goes in v2:
time: 307 us; the launch traced here: 306 us
  blocking collectives  204 us (66%)
  Pallas kernels  47.7 us (16%)
  starting transfers between devices  27 us (9%)
  waiting for transfers between devices  24 us (8%)
    all_to_all x4, blocking collectives, everywhere(): return lax.all_to_all(merge(over_plane), 'z', 0, 0, tiled=True)  137 us
    all_to_all x5, blocking collectives, everywhere(): over_plane = lax.all_to_all(note, plane, 0, 0, tiled=True)  66.7 us
    pallas_call x4, Pallas kernels, per_device(): *result, note, guess, known = again(everywhere(note), guess, known, fields)  30.9 us
    all_to_all x1, waiting for transfers between devices, everywhere(): return lax.all_to_all(merge(over_plane), 'z', 0, 0, tiled=True)  21.1 us
    ppermute x1, starting transfers between devices, per_device(): lax.ppermute(first, ROW, down)  16 us
    pallas_call x5, Pallas kernels, everywhere(): return lax.all_to_all(merge(over_plane), 'z', 0, 0, tiled=True)  7.71 us
  transfers between devices with their start and end apart: 5, of which 3 were waited for; matrix products, arithmetic and copies ran while one was open for 0% of the time, Pallas kernels for 0%

profile of v2, /device:TPU:1, one launch (start us, length us, event | category | flops | bytes accessed | tf_op | source)
XLA Modules:
  0.0 306.0 jit_solution(1078279621063296939)
XLA Ops:
  0.6 2.3 prepare.1
  2.9 16.0 %collective-permute-start = (f32[6,12,128]{2,1,0:T(8,128)}, f32[6,12,128]{2,1,0:T(8,128)S(1)}, u32[]{:S(2)}, u32[]{:S(2)}) collective-permute-start(f32[6,12,128]{2,1,0:T(8,128)} %get-tuple-element.81), channel_id=1, source_target_pairs={{16,0},{32,16},{48,32},{64,48},{80,64},{96,80},{112,96},{128,112},... | collective-permute-start | bytes 110600 | tf_op jit(solution)/shard_map/ppermute | solution.py:376
  19.0 1.9 collective-permute-start.1
  20.9 0.0 collective-permute-done.after
  20.9 0.0 copy-start
  20.9 1.5 collective-permute-done.1.before
  22.4 0.0 copy-start.1
  22.4 0.0 copy-done
  22.4 0.6 copy-done.1
  23.0 1.8 edges.1
  24.7 1.3 collective-permute-start.2
  26.0 4.0 %collective-permute-start.3 = (f32[88,128]{1,0:T(8,128)}, f32[88,128]{1,0:T(8,128)S(1)}, u32[]{:S(2)}, u32[]{:S(2)}) collective-permute-start(f32[88,128]{1,0:T(8,128)} %get-tuple-element.85), channel_id=1, source_target_pairs={{0,1},{1,2},{2,3},{3,4},{4,5},{5,6},{6,7},{7,8},{8,9},{9,10},{10,1... | collective-permute-start | bytes 135176 | tf_op jit(solution)/shard_map/ppermute | solution.py:385
  30.0 0.0 collective-permute-done.2.refs_1_
  30.0 0.0 copy-start.2
  30.1 1.4 collective-permute-done.3.refs_2_
  31.5 0.0 copy-start.3
  31.5 0.0 copy-done.2
  31.5 0.6 copy-done.3
  32.1 5.0 %first_run.1 = (f32[6,88,256]{2,1,0:T(8,128)S(1)}, f32[64,128]{1,0:T(8,128)}, f32[64,128]{1,0:T(8,128)}, f32[64,128]{1,0:T(8,128)}, f32[32,1,128]{2,1,0:T(1,128)}, /*index=5*/f32[1,128]{1,0:T(1,128)}, s32[1]{0:T(128)}) custom-call(f32[6,88,128]{2,1,0:T(8,128)} %get-tuple-element.83.refs_0_, f32[88,128]{1,0:T(8,128)} %copy-done.2, f32[88,128]{1,0:T(8,128)} %copy-done.3), custom_call_target="tpu_custom_call" | custom-call | tf_op jit(solution)/shard_map/first_run/pallas_call | solution.py:423
  37.1 12.3 %all_to_all.62.notes = f32[32,1,128]{2,1,0:T(1,128)} all-to-all(f32[32,1,128]{2,1,0:T(1,128)} %get-tuple-element.86), channel_id=1, replica_groups=mesh['z'=32,'core'=2,'col'=16] {'core','col'}, dimensions={0} | all-to-all | bytes 32768 | tf_op jit(solution)/shard_map/all_to_all | solution.py:388
  49.4 1.3 merge_notes.6
  50.7 46.0 %all_to_all.63.refs_0_ = f32[32,1,128]{2,1,0:T(1,128)} all-to-all(f32[32,1,128]{2,1,0:T(1,128)} %merge_notes.6), channel_id=1, replica_groups=mesh['z'=32,'core'=2,'col'=16] {'z'}, dimensions={0} | all-to-all | bytes 32768 | tf_op jit(solution)/shard_map/all_to_all | solution.py:390
  96.7 7.1 %second_run.1 = (f32[64,128]{1,0:T(8,128)}, f32[64,128]{1,0:T(8,128)}, f32[64,128]{1,0:T(8,128)}, f32[32,1,640]{2,1,0:T(1,128)}, f32[1,128]{1,0:T(1,128)}, /*index=5*/s32[1]{0:T(128)}) custom-call(f32[32,1,128]{2,1,0:T(1,128)} %all_to_all.63.refs_0_, f32[1,128]{1,0:T(1,128)} %get-tuple-element.87.refs_1_, s32[1]{0:T(128)} %get-tuple-element.88.refs_2_, ...), custom_call_target="tpu_custom_call" | custom-call | tf_op jit(solution)/shard_map/second_run/pallas_call | solution.py:431
  103.8 13.6 %all_to_all.64.notes = f32[32,1,640]{2,1,0:T(1,128)} all-to-all(f32[32,1,640]{2,1,0:T(1,128)} %get-tuple-element.90), channel_id=1, replica_groups=mesh['z'=32,'core'=2,'col'=16] {'core','col'}, dimensions={0} | all-to-all | bytes 163840 | tf_op jit(solution)/shard_map/all_to_all | solution.py:388
  117.3 1.7 merge_notes.7
  119.0 30.4 %all_to_all.65.refs_0_ = f32[32,1,640]{2,1,0:T(1,128)} all-to-all(f32[32,1,640]{2,1,0:T(1,128)} %merge_notes.7), channel_id=1, replica_groups=mesh['z'=32,'core'=2,'col'=16] {'z'}, dimensions={0} | all-to-all | bytes 163840 | tf_op jit(solution)/shard_map/all_to_all | solution.py:390
  149.4 8.6 %third_run.1 = (f32[64,128]{1,0:T(8,128)}, f32[64,128]{1,0:T(8,128)}, f32[64,128]{1,0:T(8,128)}, f32[32,1,640]{2,1,0:T(1,128)}, f32[1,128]{1,0:T(1,128)}, /*index=5*/s32[1]{0:T(128)}) custom-call(f32[32,1,640]{2,1,0:T(1,128)} %all_to_all.65.refs_0_, f32[1,128]{1,0:T(1,128)} %get-tuple-element.91.refs_1_, s32[1]{0:T(128)} %get-tuple-element.92.refs_2_, ...), custom_call_target="tpu_custom_call" | custom-call | tf_op jit(solution)/shard_map/third_run/pallas_call | solution.py:431
  158.1 13.7 %all_to_all.66.notes = f32[32,1,640]{2,1,0:T(1,128)} all-to-all(f32[32,1,640]{2,1,0:T(1,128)} %get-tuple-element.93), channel_id=1, replica_groups=mesh['z'=32,'core'=2,'col'=16] {'core','col'}, dimensions={0} | all-to-all | bytes 163840 | tf_op jit(solution)/shard_map/all_to_all | solution.py:388
  171.8 1.7 merge_notes.8
  173.5 30.4 %all_to_all.67.refs_0_ = f32[32,1,640]{2,1,0:T(1,128)} all-to-all(f32[32,1,640]{2,1,0:T(1,128)} %merge_notes.8), channel_id=1, replica_groups=mesh['z'=32,'core'=2,'col'=16] {'z'}, dimensions={0} | all-to-all | bytes 163840 | tf_op jit(solution)/shard_map/all_to_all | solution.py:390
  203.9 8.5 %later_run.2 = (f32[64,128]{1,0:T(8,128)}, f32[64,128]{1,0:T(8,128)}, f32[64,128]{1,0:T(8,128)}, f32[32,1,640]{2,1,0:T(1,128)}, f32[1,128]{1,0:T(1,128)}, /*index=5*/s32[1]{0:T(128)}) custom-call(f32[32,1,640]{2,1,0:T(1,128)} %all_to_all.67.refs_0_, f32[1,128]{1,0:T(1,128)} %get-tuple-element.94.refs_1_, s32[1]{0:T(128)} %get-tuple-element.95.refs_2_, ...), custom_call_target="tpu_custom_call" | custom-call | tf_op jit(solution)/shard_map/later_run/pallas_call | solution.py:431
  212.4 13.7 %all_to_all.68.notes = f32[32,1,640]{2,1,0:T(1,128)} all-to-all(f32[32,1,640]{2,1,0:T(1,128)} %get-tuple-element.96), channel_id=1, replica_groups=mesh['z'=32,'core'=2,'col'=16] {'core','col'}, dimensions={0} | all-to-all | bytes 163840 | tf_op jit(solution)/shard_map/all_to_all | solution.py:388
  226.1 1.7 merge_notes.9
  227.8 30.4 %all_to_all.69.refs_0_ = f32[32,1,640]{2,1,0:T(1,128)} all-to-all(f32[32,1,640]{2,1,0:T(1,128)} %merge_notes.9), channel_id=1, replica_groups=mesh['z'=32,'core'=2,'col'=16] {'z'}, dimensions={0} | all-to-all | bytes 163840 | tf_op jit(solution)/shard_map/all_to_all | solution.py:390
  258.2 6.7 %check_run.1 = (f32[64,128]{1,0:T(8,128)}, f32[64,128]{1,0:T(8,128)}, f32[64,128]{1,0:T(8,128)}, f32[32,1,128]{2,1,0:T(1,128)}, f32[1,128]{1,0:T(1,128)S(1)}, /*index=5*/s32[1]{0:T(128)}) custom-call(f32[32,1,640]{2,1,0:T(1,128)} %all_to_all.69.refs_0_, f32[1,128]{1,0:T(1,128)} %get-tuple-element.97.refs_1_, s32[1]{0:T(128)} %get-tuple-element.98.refs_2_, ...), custom_call_target="tpu_custom_call" | custom-call | tf_op jit(solution)/shard_map/check_run/pallas_call | solution.py:431
  264.9 13.4 %all_to_all.70.notes = f32[32,1,128]{2,1,0:T(1,128)} all-to-all(f32[32,1,128]{2,1,0:T(1,128)} %get-tuple-element.99), channel_id=1, replica_groups=mesh['z'=32,'core'=2,'col'=16] {'core','col'}, dimensions={0} | all-to-all | bytes 32768 | tf_op jit(solution)/shard_map/all_to_all | solution.py:388
  278.3 1.3 merge_notes.10
  279.7 3.8 %all-to-all-start.11 = ((f32[32,1,128]{2,1,0:T(1,128)}), f32[32,1,128]{2,1,0:T(1,128)S(1)}, u32[]{:S(2)}, u32[]{:S(2)}) async-start(f32[32,1,128]{2,1,0:T(1,128)} %merge_notes.10), calls=%async_computation.11 | async-start | bytes 32768 | tf_op jit(solution)/shard_map/all_to_all | solution.py:390
  283.5 21.1 %all-to-all-done.11 = f32[32,1,128]{2,1,0:T(1,128)S(1)} async-done(((f32[32,1,128]{2,1,0:T(1,128)}), f32[32,1,128]{2,1,0:T(1,128)S(1)}, u32[]{:S(2)}, u32[]{:S(2)}) %all-to-all-start.11) | async-done | bytes 16416 | tf_op jit(solution)/shard_map/all_to_all | solution.py:390
  304.6 0.1 slice_reduce_fusion.1
  304.7 0.7 compare_reduce_fusion.1
  305.4 0.6 while.22
  (1 shorter events, 0.0 us)
Async XLA Ops:
  2.9 18.0 %collective-permute-start = (f32[6,12,128]{2,1,0:T(8,128)}, f32[6,12,128]{2,1,0:T(8,128)S(1)}, u32[]{:S(2)}, u32[]{:S(2)}) collective-permute-start(f32[6,12,128]{2,1,0:T(8,128)} %get-tuple-element.81), channel_id=1, source_target_pairs={{16,0},{32,16},{48,32},{64,48},{80,64},{96,80},{112,96},{128,112},... | collective-permute-start | bytes 110600 | tf_op jit(solution)/shard_map/ppermute | solution.py:376
  19.0 3.4 %collective-permute-start.1 = (f32[6,12,128]{2,1,0:T(8,128)}, f32[6,12,128]{2,1,0:T(8,128)S(1)}, u32[]{:S(2)}, u32[]{:S(2)}) collective-permute-start(f32[6,12,128]{2,1,0:T(8,128)} %get-tuple-element.82), channel_id=1, source_target_pairs={{0,16},{16,32},{32,48},{48,64},{64,80},{80,96},{96,112},{112,128},... | collective-permute-start | bytes 110600 | tf_op jit(solution)/shard_map/ppermute | solution.py:376
  20.9 1.5 copy-start
  22.4 0.6 copy-start.1
  24.7 5.3 %collective-permute-start.2 = (f32[88,128]{1,0:T(8,128)}, f32[88,128]{1,0:T(8,128)S(1)}, u32[]{:S(2)}, u32[]{:S(2)}) collective-permute-start(f32[88,128]{1,0:T(8,128)} %get-tuple-element.84), channel_id=1, source_target_pairs={{1,0},{2,1},{3,2},{4,3},{5,4},{6,5},{7,6},{8,7},{9,8},{10,9},{11,1... | collective-permute-start | bytes 135176 | tf_op jit(solution)/shard_map/ppermute | solution.py:385
  26.0 5.4 %collective-permute-start.3 = (f32[88,128]{1,0:T(8,128)}, f32[88,128]{1,0:T(8,128)S(1)}, u32[]{:S(2)}, u32[]{:S(2)}) collective-permute-start(f32[88,128]{1,0:T(8,128)} %get-tuple-element.85), channel_id=1, source_target_pairs={{0,1},{1,2},{2,3},{3,4},{4,5},{5,6},{6,7},{7,8},{8,9},{9,10},{10,1... | collective-permute-start | bytes 135176 | tf_op jit(solution)/shard_map/ppermute | solution.py:385
  30.0 1.4 copy-start.2
  31.5 0.6 copy-start.3
  279.7 24.9 %all-to-all-start.11 = ((f32[32,1,128]{2,1,0:T(1,128)}), f32[32,1,128]{2,1,0:T(1,128)S(1)}, u32[]{:S(2)}, u32[]{:S(2)}) async-start(f32[32,1,128]{2,1,0:T(1,128)} %merge_notes.10), calls=%async_computation.11 | async-start | bytes 32768 | tf_op jit(solution)/shard_map/all_to_all | solution.py:390

commit v3 on v2

--- a/solution.py
+++ b/solution.py
@@ -121,23 +121,22 @@
     )
 
 
-def face_flux(flow_old, surface, surf_high, bed_max, rough, opening, time_step):
+def face_flux(flow_old, surface, surf_high, bed_max, drag, opening, pull):
     flow_depth = jnp.maximum(surface, surf_high) - bed_max
     driving = jnp.maximum(flow_depth, 0.0)
     friction_depth = jnp.maximum(flow_depth, FLOW_FLOOR)
-    slope = (surf_high - surface) / SPACING
-    driven = flow_old - GRAVITY * driving * time_step * slope
-    damping = 1.0 + GRAVITY * time_step * rough * jnp.abs(flow_old) * jnp.exp(
-        -7.0 / 3.0 * jnp.log(friction_depth)
-    )
+    driven = flow_old - (surf_high - surface) * pull * driving
+    damping = 1.0 + drag * jnp.abs(flow_old) * jnp.exp(-7.0 / 3.0 * jnp.log(friction_depth))
     return opening * driven / damping
 
 
 def advance(depth, flow_x, flow_y, bed, rough, faces, time_step):
     surface = depth + bed
     (bed_x, open_x), (bed_y, open_y) = faces
-    rows_new = face_flux(flow_x, surface, next_of(surface, 0), bed_x, rough, open_x, time_step)
-    cols_new = face_flux(flow_y, surface, next_of(surface, 1), bed_y, rough, open_y, time_step)
+    drag = GRAVITY * time_step * rough
+    pull = GRAVITY / SPACING * time_step
+    rows_new = face_flux(flow_x, surface, next_of(surface, 0), bed_x, drag, open_x, pull)
+    cols_new = face_flux(flow_y, surface, next_of(surface, 1), bed_y, drag, open_y, pull)
     change = previous_of(rows_new, 0) - rows_new + (previous_of(cols_new, 1) - cols_new)
     return jnp.maximum(depth + time_step / SPACING * change, 0.0), rows_new, cols_new
 
@@ -241,7 +240,7 @@
         join(fields, tall, after, before)
     else:
         notes, guess_in, known_in, fields, depth_out, flow_x_out, flow_y_out, note_out, guess_out, known_out = refs[:10]
-    state, faces, saved, guesses, depths, spots = refs[-6:]
+    state, faces, saved, times, depths, spots = refs[-6:]
     rows, cols = tile
     line_lane = lanes_of((1, 128))
 
@@ -279,7 +278,7 @@
         square = (16, 128)
         onto = rows_of(square) == lanes_of(square)
         spread = jnp.sum(jnp.where(onto, jnp.broadcast_to(guess, square), 0.0), axis=1, keepdims=True)
-        guesses[...] = jnp.broadcast_to(spread, square)
+        times[...] = jnp.broadcast_to(step_of(spread), times.shape)
     known_out[0] = known if writes or first else jnp.int32(UNUSED)
 
     for f in range(3):
@@ -314,7 +313,7 @@
                 cell = (rows_of((rows, cols)) * cols + lanes_of((rows, cols))).astype(jnp.float32)
                 spots[j] = jnp.min(jnp.where(own == deepest, cell, 1.0 * (rows * cols - 1))).astype(jnp.int32)
 
-        level = deepest if first else guesses[pl.ds(step, 1), :][:, :1]
+        time_step = step_of(deepest) if first else times[pl.ds(step, 1), :]
         new = advance(
             depth,
             flow_x,
@@ -322,7 +321,7 @@
             fields[3],
             fields[4],
             ((faces[0], faces[1]), (faces[2], faces[3])),
-            step_of(level),
+            time_step,
         )
         for f in range(3):
             state[f] = new[f]
@@ -409,7 +408,7 @@
                 pltpu.VMEM((3, *large), jnp.float32),
                 pltpu.VMEM((4, *large), jnp.float32),
                 pltpu.VMEM((FIELDS, large[0] + 8, large[1]), jnp.float32),
-                pltpu.VMEM((16, 128), jnp.float32),
+                pltpu.VMEM((16, large[1]), jnp.float32),
                 pltpu.VMEM((16, 128), jnp.float32),
                 pltpu.SMEM((REACH,), jnp.int32),
             ],

time: 307 us -> 307 us (level)
  no operation moved by 1% of the time
where the time goes in v3:
time: 307 us; the launch traced here: 305 us
  blocking collectives  204 us (66%)
  Pallas kernels  47 us (15%)
  starting transfers between devices  27 us (9%)
  waiting for transfers between devices  24 us (8%)
    all_to_all x4, blocking collectives, everywhere(): return lax.all_to_all(merge(over_plane), 'z', 0, 0, tiled=True)  137 us
    all_to_all x5, blocking collectives, everywhere(): over_plane = lax.all_to_all(note, plane, 0, 0, tiled=True)  66.7 us
    pallas_call x4, Pallas kernels, per_device(): *result, note, guess, known = again(everywhere(note), guess, known, fields)  30.4 us
    all_to_all x1, waiting for transfers between devices, everywhere(): return lax.all_to_all(merge(over_plane), 'z', 0, 0, tiled=True)  21.1 us
    ppermute x1, starting transfers between devices, per_device(): lax.ppermute(first, ROW, down)  16 us
    pallas_call x5, Pallas kernels, everywhere(): return lax.all_to_all(merge(over_plane), 'z', 0, 0, tiled=True)  7.71 us
  transfers between devices with their start and end apart: 5, of which 3 were waited for; matrix products, arithmetic and copies ran while one was open for 0% of the time, Pallas kernels for 0%

profile of v3, /device:TPU:1, one launch (start us, length us, event | category | flops | bytes accessed | tf_op | source)
XLA Modules:
  0.0 305.3 jit_solution(5881556734791942036)
XLA Ops:
  0.6 2.3 prepare.1
  2.9 16.0 %collective-permute-start = (f32[6,12,128]{2,1,0:T(8,128)}, f32[6,12,128]{2,1,0:T(8,128)S(1)}, u32[]{:S(2)}, u32[]{:S(2)}) collective-permute-start(f32[6,12,128]{2,1,0:T(8,128)} %get-tuple-element.81), channel_id=1, source_target_pairs={{16,0},{32,16},{48,32},{64,48},{80,64},{96,80},{112,96},{128,112},... | collective-permute-start | bytes 110600 | tf_op jit(solution)/shard_map/ppermute | solution.py:375
  19.0 1.9 collective-permute-start.1
  20.9 0.0 collective-permute-done.after
  20.9 0.0 copy-start
  20.9 1.5 collective-permute-done.1.before
  22.4 0.0 copy-start.1
  22.4 0.0 copy-done
  22.4 0.6 copy-done.1
  23.0 1.8 edges.1
  24.7 1.3 collective-permute-start.2
  26.0 4.0 %collective-permute-start.3 = (f32[88,128]{1,0:T(8,128)}, f32[88,128]{1,0:T(8,128)S(1)}, u32[]{:S(2)}, u32[]{:S(2)}) collective-permute-start(f32[88,128]{1,0:T(8,128)} %get-tuple-element.85), channel_id=1, source_target_pairs={{0,1},{1,2},{2,3},{3,4},{4,5},{5,6},{6,7},{7,8},{8,9},{9,10},{10,1... | collective-permute-start | bytes 135176 | tf_op jit(solution)/shard_map/ppermute | solution.py:384
  30.0 0.0 collective-permute-done.2.refs_1_
  30.0 0.0 copy-start.2
  30.1 1.4 collective-permute-done.3.refs_2_
  31.5 0.0 copy-start.3
  31.5 0.0 copy-done.2
  31.5 0.6 copy-done.3
  32.1 4.8 %first_run.1 = (f32[6,88,256]{2,1,0:T(8,128)S(1)}, f32[64,128]{1,0:T(8,128)}, f32[64,128]{1,0:T(8,128)}, f32[64,128]{1,0:T(8,128)}, f32[32,1,128]{2,1,0:T(1,128)}, /*index=5*/f32[1,128]{1,0:T(1,128)}, s32[1]{0:T(128)}) custom-call(f32[6,88,128]{2,1,0:T(8,128)} %get-tuple-element.83.refs_0_, f32[88,128]{1,0:T(8,128)} %copy-done.2, f32[88,128]{1,0:T(8,128)} %copy-done.3), custom_call_target="tpu_custom_call" | custom-call | tf_op jit(solution)/shard_map/first_run/pallas_call | solution.py:422
  36.9 12.3 %all_to_all.62.notes = f32[32,1,128]{2,1,0:T(1,128)} all-to-all(f32[32,1,128]{2,1,0:T(1,128)} %get-tuple-element.86), channel_id=1, replica_groups=mesh['z'=32,'core'=2,'col'=16] {'core','col'}, dimensions={0} | all-to-all | bytes 32768 | tf_op jit(solution)/shard_map/all_to_all | solution.py:387
  49.2 1.3 merge_notes.6
  50.5 46.0 %all_to_all.63.refs_0_ = f32[32,1,128]{2,1,0:T(1,128)} all-to-all(f32[32,1,128]{2,1,0:T(1,128)} %merge_notes.6), channel_id=1, replica_groups=mesh['z'=32,'core'=2,'col'=16] {'z'}, dimensions={0} | all-to-all | bytes 32768 | tf_op jit(solution)/shard_map/all_to_all | solution.py:389
  96.5 6.9 %second_run.1 = (f32[64,128]{1,0:T(8,128)}, f32[64,128]{1,0:T(8,128)}, f32[64,128]{1,0:T(8,128)}, f32[32,1,640]{2,1,0:T(1,128)}, f32[1,128]{1,0:T(1,128)}, /*index=5*/s32[1]{0:T(128)}) custom-call(f32[32,1,128]{2,1,0:T(1,128)} %all_to_all.63.refs_0_, f32[1,128]{1,0:T(1,128)} %get-tuple-element.87.refs_1_, s32[1]{0:T(128)} %get-tuple-element.88.refs_2_, ...), custom_call_target="tpu_custom_call" | custom-call | tf_op jit(solution)/shard_map/second_run/pallas_call | solution.py:430
  103.4 13.6 %all_to_all.64.notes = f32[32,1,640]{2,1,0:T(1,128)} all-to-all(f32[32,1,640]{2,1,0:T(1,128)} %get-tuple-element.90), channel_id=1, replica_groups=mesh['z'=32,'core'=2,'col'=16] {'core','col'}, dimensions={0} | all-to-all | bytes 163840 | tf_op jit(solution)/shard_map/all_to_all | solution.py:387
  117.0 1.7 merge_notes.7
  118.7 30.4 %all_to_all.65.refs_0_ = f32[32,1,640]{2,1,0:T(1,128)} all-to-all(f32[32,1,640]{2,1,0:T(1,128)} %merge_notes.7), channel_id=1, replica_groups=mesh['z'=32,'core'=2,'col'=16] {'z'}, dimensions={0} | all-to-all | bytes 163840 | tf_op jit(solution)/shard_map/all_to_all | solution.py:389
  149.1 8.5 %third_run.1 = (f32[64,128]{1,0:T(8,128)}, f32[64,128]{1,0:T(8,128)}, f32[64,128]{1,0:T(8,128)}, f32[32,1,640]{2,1,0:T(1,128)}, f32[1,128]{1,0:T(1,128)}, /*index=5*/s32[1]{0:T(128)}) custom-call(f32[32,1,640]{2,1,0:T(1,128)} %all_to_all.65.refs_0_, f32[1,128]{1,0:T(1,128)} %get-tuple-element.91.refs_1_, s32[1]{0:T(128)} %get-tuple-element.92.refs_2_, ...), custom_call_target="tpu_custom_call" | custom-call | tf_op jit(solution)/shard_map/third_run/pallas_call | solution.py:430
  157.6 13.7 %all_to_all.66.notes = f32[32,1,640]{2,1,0:T(1,128)} all-to-all(f32[32,1,640]{2,1,0:T(1,128)} %get-tuple-element.93), channel_id=1, replica_groups=mesh['z'=32,'core'=2,'col'=16] {'core','col'}, dimensions={0} | all-to-all | bytes 163840 | tf_op jit(solution)/shard_map/all_to_all | solution.py:387
  171.3 1.7 merge_notes.8
  173.0 30.4 %all_to_all.67.refs_0_ = f32[32,1,640]{2,1,0:T(1,128)} all-to-all(f32[32,1,640]{2,1,0:T(1,128)} %merge_notes.8), channel_id=1, replica_groups=mesh['z'=32,'core'=2,'col'=16] {'z'}, dimensions={0} | all-to-all | bytes 163840 | tf_op jit(solution)/shard_map/all_to_all | solution.py:389
  203.4 8.4 %later_run.2 = (f32[64,128]{1,0:T(8,128)}, f32[64,128]{1,0:T(8,128)}, f32[64,128]{1,0:T(8,128)}, f32[32,1,640]{2,1,0:T(1,128)}, f32[1,128]{1,0:T(1,128)}, /*index=5*/s32[1]{0:T(128)}) custom-call(f32[32,1,640]{2,1,0:T(1,128)} %all_to_all.67.refs_0_, f32[1,128]{1,0:T(1,128)} %get-tuple-element.94.refs_1_, s32[1]{0:T(128)} %get-tuple-element.95.refs_2_, ...), custom_call_target="tpu_custom_call" | custom-call | tf_op jit(solution)/shard_map/later_run/pallas_call | solution.py:430
  211.8 13.7 %all_to_all.68.notes = f32[32,1,640]{2,1,0:T(1,128)} all-to-all(f32[32,1,640]{2,1,0:T(1,128)} %get-tuple-element.96), channel_id=1, replica_groups=mesh['z'=32,'core'=2,'col'=16] {'core','col'}, dimensions={0} | all-to-all | bytes 163840 | tf_op jit(solution)/shard_map/all_to_all | solution.py:387
  225.5 1.7 merge_notes.9
  227.2 30.4 %all_to_all.69.refs_0_ = f32[32,1,640]{2,1,0:T(1,128)} all-to-all(f32[32,1,640]{2,1,0:T(1,128)} %merge_notes.9), channel_id=1, replica_groups=mesh['z'=32,'core'=2,'col'=16] {'z'}, dimensions={0} | all-to-all | bytes 163840 | tf_op jit(solution)/shard_map/all_to_all | solution.py:389
  257.6 6.6 %check_run.1 = (f32[64,128]{1,0:T(8,128)}, f32[64,128]{1,0:T(8,128)}, f32[64,128]{1,0:T(8,128)}, f32[32,1,128]{2,1,0:T(1,128)}, f32[1,128]{1,0:T(1,128)S(1)}, /*index=5*/s32[1]{0:T(128)}) custom-call(f32[32,1,640]{2,1,0:T(1,128)} %all_to_all.69.refs_0_, f32[1,128]{1,0:T(1,128)} %get-tuple-element.97.refs_1_, s32[1]{0:T(128)} %get-tuple-element.98.refs_2_, ...), custom_call_target="tpu_custom_call" | custom-call | tf_op jit(solution)/shard_map/check_run/pallas_call | solution.py:430
  264.2 13.4 %all_to_all.70.notes = f32[32,1,128]{2,1,0:T(1,128)} all-to-all(f32[32,1,128]{2,1,0:T(1,128)} %get-tuple-element.99), channel_id=1, replica_groups=mesh['z'=32,'core'=2,'col'=16] {'core','col'}, dimensions={0} | all-to-all | bytes 32768 | tf_op jit(solution)/shard_map/all_to_all | solution.py:387
  277.6 1.3 merge_notes.10
  279.0 3.8 %all-to-all-start.11 = ((f32[32,1,128]{2,1,0:T(1,128)}), f32[32,1,128]{2,1,0:T(1,128)S(1)}, u32[]{:S(2)}, u32[]{:S(2)}) async-start(f32[32,1,128]{2,1,0:T(1,128)} %merge_notes.10), calls=%async_computation.11 | async-start | bytes 32768 | tf_op jit(solution)/shard_map/all_to_all | solution.py:389
  282.8 21.1 %all-to-all-done.11 = f32[32,1,128]{2,1,0:T(1,128)S(1)} async-done(((f32[32,1,128]{2,1,0:T(1,128)}), f32[32,1,128]{2,1,0:T(1,128)S(1)}, u32[]{:S(2)}, u32[]{:S(2)}) %all-to-all-start.11) | async-done | bytes 16416 | tf_op jit(solution)/shard_map/all_to_all | solution.py:389
  303.9 0.1 slice_reduce_fusion.1
  303.9 0.7 compare_reduce_fusion.1
  304.6 0.6 while.22
  (1 shorter events, 0.0 us)
Async XLA Ops:
  2.9 18.0 %collective-permute-start = (f32[6,12,128]{2,1,0:T(8,128)}, f32[6,12,128]{2,1,0:T(8,128)S(1)}, u32[]{:S(2)}, u32[]{:S(2)}) collective-permute-start(f32[6,12,128]{2,1,0:T(8,128)} %get-tuple-element.81), channel_id=1, source_target_pairs={{16,0},{32,16},{48,32},{64,48},{80,64},{96,80},{112,96},{128,112},... | collective-permute-start | bytes 110600 | tf_op jit(solution)/shard_map/ppermute | solution.py:375
  19.0 3.4 %collective-permute-start.1 = (f32[6,12,128]{2,1,0:T(8,128)}, f32[6,12,128]{2,1,0:T(8,128)S(1)}, u32[]{:S(2)}, u32[]{:S(2)}) collective-permute-start(f32[6,12,128]{2,1,0:T(8,128)} %get-tuple-element.82), channel_id=1, source_target_pairs={{0,16},{16,32},{32,48},{48,64},{64,80},{80,96},{96,112},{112,128},... | collective-permute-start | bytes 110600 | tf_op jit(solution)/shard_map/ppermute | solution.py:375
  20.9 1.5 copy-start
  22.4 0.6 copy-start.1
  24.7 5.3 %collective-permute-start.2 = (f32[88,128]{1,0:T(8,128)}, f32[88,128]{1,0:T(8,128)S(1)}, u32[]{:S(2)}, u32[]{:S(2)}) collective-permute-start(f32[88,128]{1,0:T(8,128)} %get-tuple-element.84), channel_id=1, source_target_pairs={{1,0},{2,1},{3,2},{4,3},{5,4},{6,5},{7,6},{8,7},{9,8},{10,9},{11,1... | collective-permute-start | bytes 135176 | tf_op jit(solution)/shard_map/ppermute | solution.py:384
  26.0 5.4 %collective-permute-start.3 = (f32[88,128]{1,0:T(8,128)}, f32[88,128]{1,0:T(8,128)S(1)}, u32[]{:S(2)}, u32[]{:S(2)}) collective-permute-start(f32[88,128]{1,0:T(8,128)} %get-tuple-element.85), channel_id=1, source_target_pairs={{0,1},{1,2},{2,3},{3,4},{4,5},{5,6},{6,7},{7,8},{8,9},{9,10},{10,1... | collective-permute-start | bytes 135176 | tf_op jit(solution)/shard_map/ppermute | solution.py:384
  30.0 1.4 copy-start.2
  31.5 0.6 copy-start.3
  279.0 24.9 %all-to-all-start.11 = ((f32[32,1,128]{2,1,0:T(1,128)}), f32[32,1,128]{2,1,0:T(1,128)S(1)}, u32[]{:S(2)}, u32[]{:S(2)}) async-start(f32[32,1,128]{2,1,0:T(1,128)} %merge_notes.10), calls=%async_computation.11 | async-start | bytes 32768 | tf_op jit(solution)/shard_map/all_to_all | solution.py:389
